TPU v7x, 128 devices: a whole 4x4x4 slice. The times are simulated.
128 devices in a mesh: group: 8 (over y, core), member: 16 (over z, x).
Axes of the slice: x: 4, y: 4, z: 4, core: 2. Of those that a mesh axis runs over, the one named last changes fastest.
Arguments:
- volume_frac: float32 [512, 1024, 256], P('group', 'member'), may hold values from 0 to 1
- velocity: bfloat16 [3, 512, 1024, 256], P(None, 'group', 'member'), may hold values from -6 to 6
- drop_block: int32 [8, 16, 16], P('group', 'member'), may hold values from 0 to 255, as said below
- drop_owner: int32 [8, 16, 16, 1], P('group', 'member'), may hold values from 0 to 15; in each aligned block of 16 rows (0 to 15, 16 to 31, ..., all dimensions but the last counted through in order) at most 2 rows name the same one
- parcel_vel: float32 [8, 16, 16, 2, 3, 512], P('group', 'member'), may hold values from -6 to 6
- parcel_rate: float32 [8, 16, 16, 2, 512], P('group', 'member'), may hold values from 0.05 to 0.8
- parcel_weight: float32 [8, 16, 16, 2, 512], P('group', 'member'), may hold values from 0.3 to 3
- parcel_cell: int32 [8, 16, 16, 2, 512], P('group', 'member'), may hold values from 0 to 4095
Outputs:
- frac_next: float32 [512, 1024, 256], P('group', 'member')
- velocity_next: bfloat16 [3, 512, 1024, 256], P(None, 'group', 'member')
- parcel_next: float32 [8, 16, 16, 2, 3, 512], P('group', 'member')
Inputs may be any that keep to these rules, and one draw needn't show every extreme that they name: `drop_block`: the 16 entries of one device are distinct. `drop_owner`: no owner gets more than 2 of one device's droplet blocks; some device sends exactly 2 to one owner.
All inputs are finite; a program needn't handle non-finite values.
Results may differ from a plain program's by a relative error of at most 0.001.
Values may be sent and summed in bfloat16 or wider, within the bound.
A program may use at most 448 MiB of HBM per device.

v0:
```python
import jax
import jax.numpy as jnp
from jax import lax
from jax.sharding import PartitionSpec as P

CAP = 2


courant = 0.025


def padded_2(cells, sides, width):
    for axis, dim in sides:
        count = lax.axis_size(axis)
        ends = count - 1
        head = lax.slice_in_dim(cells, 0, width, axis=dim)
        tail = lax.slice_in_dim(cells, cells.shape[dim] - width, cells.shape[dim], axis=dim)
        cells = jnp.concatenate(
            [
                lax.ppermute(tail, axis, [(i, (i + 1) % count) for i in range(ends)]),
                cells,
                lax.ppermute(head, axis, [((i + 1) % count, i) for i in range(ends)]),
            ],
            axis=dim,
        )
    return cells


def face_div(frac_pad, speed_pad, along):
    inner = [slice(1, -1)] * 3
    lower_cut = list(inner)
    lower_cut[along] = slice(0, -1)
    upper_cut = list(inner)
    upper_cut[along] = slice(1, None)
    left_frac = frac_pad[tuple(lower_cut)]
    right_frac = frac_pad[tuple(upper_cut)]
    left_speed = speed_pad[tuple(lower_cut)]
    face_flux = courant * (
        jnp.maximum(left_speed, 0.0) * left_frac + jnp.minimum(left_speed, 0.0) * right_frac
    )
    length = face_flux.shape[along]
    return lax.slice_in_dim(face_flux, 1, length, axis=along) - lax.slice_in_dim(
        face_flux, 0, length - 1, axis=along
    )


def one_slot(block_data, filled, parcel_v, drag_rate, weight, cell_ids):
    onehot = (cell_ids[:, None] == lax.iota(jnp.int32, 4096)[None, :]).astype(jnp.bfloat16)
    sampled = jnp.einsum("kc,pc->kp", block_data, onehot, preferred_element_type=jnp.float32)
    gas_share = 1.0 - sampled[3]
    acceleration = filled.astype(jnp.float32) * drag_rate * gas_share * (sampled[:3] - parcel_v)
    deposit_w = (weight * acceleration).astype(jnp.bfloat16)
    source = jnp.einsum("kp,pc->kc", deposit_w, onehot, preferred_element_type=jnp.float32)
    return (parcel_v + acceleration, source.astype(jnp.bfloat16))


def spray_work(block_data, filled, parcel_v, drag_rate, weight, cell_ids):
    slot_count = block_data.shape[0]
    batched = (block_data, filled, parcel_v, drag_rate, weight, cell_ids)
    batched = jax.tree.map(
        lambda item: item.reshape((slot_count // 4, 4) + item.shape[1:]), batched
    )
    new_vel, source = lax.map(lambda group_items: jax.vmap(one_slot)(*group_items), batched)
    return (
        new_vel.reshape((slot_count,) + new_vel.shape[2:]),
        source.reshape((slot_count,) + source.shape[2:]),
    )


def block_corner(block_id, blocks_y, blocks_z):
    first = block_id // (blocks_y * blocks_z)
    second = block_id // blocks_z % blocks_y
    third = block_id % blocks_z
    return (first * 16, second * 16, third * 16)


def per_device(
    volume_frac,
    velocity,
    drop_block,
    drop_owner,
    parcel_vel,
    parcel_rate,
    parcel_weight,
    parcel_cell,
):
    members = lax.axis_size("member")
    cells_x, cells_y, cells_z = volume_frac.shape
    blocks_x = cells_x // 16
    blocks_y = cells_y // 16
    blocks_z = cells_z // 16
    block_total = blocks_x * blocks_y * blocks_z
    stacked = jnp.concatenate([volume_frac[None], velocity.astype(jnp.float32)], 0)
    padded = padded_2(stacked.astype(jnp.bfloat16), (("group", 1), ("member", 2)), 1).astype(
        stacked.dtype
    )
    padded = jnp.pad(padded, ((0, 0), (0, 0), (0, 0), (1, 1)))
    change = (
        face_div(padded[0], padded[1], 0)
        + face_div(padded[0], padded[2], 1)
        + face_div(padded[0], padded[3], 2)
    )
    frac_next = jnp.minimum(volume_frac - change, 1.0)
    block_ids = drop_block[0, 0]
    owners = drop_owner[0, 0, :, 0]
    drops = block_ids.shape[0]

    def fetch(block_id):
        first, second, third = block_corner(block_id, blocks_y, blocks_z)
        speeds = lax.dynamic_slice(velocity, (0, first, second, third), (3, 16, 16, 16)).reshape(
            3, 4096
        )
        fracs = lax.dynamic_slice(volume_frac, (first, second, third), (16, 16, 16)).reshape(
            1, 4096
        )
        return jnp.concatenate([speeds, fracs.astype(jnp.bfloat16)], 0)

    picked = jax.vmap(fetch)(block_ids)
    positions = lax.iota(jnp.int32, drops)
    earlier = positions[:, None] < positions[None, :]
    places = jnp.sum(((owners[:, None] == owners[None, :]) & earlier).astype(jnp.int32), axis=0)
    slot_of = owners * CAP + places
    slot_count = members * CAP
    chooser = (slot_of[None, :] == lax.iota(jnp.int32, slot_count)[:, None]).astype(jnp.bfloat16)
    outgoing = jnp.einsum(
        "sd,dkc->skc", chooser, picked, preferred_element_type=jnp.float32
    ).astype(jnp.bfloat16)
    filled = jnp.sum(chooser.astype(jnp.float32), axis=1).astype(jnp.bfloat16)
    parcels = parcel_vel.shape[-1]
    own_vel = parcel_vel[0, 0].reshape(slot_count, 3, parcels)
    own_rate = parcel_rate[0, 0].reshape(slot_count, parcels)
    own_weight = parcel_weight[0, 0].reshape(slot_count, parcels)
    own_cell = parcel_cell[0, 0].reshape(slot_count, parcels)
    received, flags_in = (
        lax.all_to_all(
            outgoing.reshape(members, CAP, 4, 4096),
            "member",
            split_axis=0,
            concat_axis=0,
            tiled=True,
        ),
        lax.all_to_all(
            filled.reshape(members, CAP), "member", split_axis=0, concat_axis=0, tiled=True
        ),
    )
    vel_out, source = spray_work(
        received.reshape(slot_count, 4, 4096),
        flags_in.reshape(slot_count),
        own_vel,
        own_rate,
        own_weight,
        own_cell,
    )
    returned = lax.all_to_all(
        source.reshape(members, CAP, 3, 4096), "member", split_axis=0, concat_axis=0, tiled=True
    ).reshape(slot_count, 3, 4096)
    block_hits = (block_ids[:, None] == lax.iota(jnp.int32, block_total)[None, :]).astype(
        jnp.bfloat16
    )
    placement = jnp.dot(chooser, block_hits, preferred_element_type=jnp.float32).astype(
        jnp.bfloat16
    )
    block_field = jnp.einsum("sb,skc->bkc", placement, returned, preferred_element_type=jnp.float32)
    block_field = block_field.reshape(blocks_x, blocks_y, blocks_z, 3, 16, 16, 16)
    drag_field = block_field.transpose(3, 0, 4, 1, 5, 2, 6).reshape(3, cells_x, cells_y, cells_z)
    velocity_next = (velocity.astype(jnp.float32) + drag_field).astype(jnp.bfloat16)
    parcel_next = vel_out.reshape(1, 1, members, CAP, 3, parcels)
    return (frac_next, velocity_next, parcel_next)


def solution(mesh):
    in_specs = (
        P("group", "member", None),
        P(None, "group", "member", None),
        P("group", "member", None),
        P("group", "member", None, None),
        P("group", "member", None, None, None, None),
        P("group", "member", None, None, None),
        P("group", "member", None, None, None),
        P("group", "member", None, None, None),
    )
    out_specs = (
        P("group", "member", None),
        P(None, "group", "member", None),
        P("group", "member", None, None, None, None),
    )
    return jax.shard_map(
        per_device, mesh=mesh, in_specs=in_specs, out_specs=out_specs, check_vma=False
    )
```

profile of v0, /device:TPU:26, one launch (start us, length us, event | category | flops | bytes accessed | tf_op | source)
XLA Modules:
  0.0 621.5 jit_solution(5728663209408651222)
XLA Ops:
  2.9 8.3 %all-to-all-start = ((bf16[16,1,2]{2,1,0:T(2,128)(2,1)}), bf16[16,1,2]{2,1,0:T(2,128)(2,1)S(1)}, u32[]{:S(2)}, u32[]{:S(2)}) async-start(bf16[16,1,2]{2,1,0:T(2,128)(2,1)} %all_to_all.16), calls=%async_computation | async-start | bytes 16384 | tf_op jit(solution)/shard_map/all_to_all | solution.py:142
  11.2 4.2 fusion.53
  21.4 69.5 %while.15 = (s32[]{:T(128)}, bf16[3,64,64,256]{3,2,1,0:T(8,128)(2,1)}, s32[16,4]{0,1:T(4,128)S(1)}, bf16[16,3,16,16,16]{4,3,2,1,0:T(8,128)(2,1)}, s32[]{:T(128)}) while((s32[]{:T(128)}, bf16[3,64,64,256]{3,2,1,0:T(8,128)(2,1)}, s32[16,4]{0,1:T(4,128)S(1)}, bf16[16,3,16,16,16]{4,3,2,1,0:T(8,128)(2,1)}, s32[]{:T(128)}) %tuple.71), condition=%wide.while_cond, body=%wide.while_body.sunk | while | flops 2 | bytes 394885 | solution.py:110
  26.4 3.7 bitcast_dynamic-update-slice_fusion.7
  30.7 3.8 bitcast_dynamic-update-slice_fusion.7
  35.2 3.8 bitcast_dynamic-update-slice_fusion.7
  39.6 3.7 bitcast_dynamic-update-slice_fusion.7
  43.9 3.7 bitcast_dynamic-update-slice_fusion.7
  48.3 3.8 bitcast_dynamic-update-slice_fusion.7
  52.7 3.7 bitcast_dynamic-update-slice_fusion.7
  57.0 3.7 bitcast_dynamic-update-slice_fusion.7
  61.4 3.7 bitcast_dynamic-update-slice_fusion.7
  74.3 3.7 bitcast_dynamic-update-slice_fusion.7
  78.6 3.7 bitcast_dynamic-update-slice_fusion.7
  82.9 3.7 bitcast_dynamic-update-slice_fusion.7
  87.3 3.7 bitcast_dynamic-update-slice_fusion.7
  91.0 67.4 %while.16 = (s32[]{:T(128)}, bf16[64,64,256]{2,1,0:T(8,128)(2,1)}, s32[16,3]{0,1:T(4,128)S(1)}, bf16[16,16,16,16]{3,2,1,0:T(8,128)(2,1)}, s32[]{:T(128)}) while((s32[]{:T(128)}, bf16[64,64,256]{2,1,0:T(8,128)(2,1)}, s32[16,3]{0,1:T(4,128)S(1)}, bf16[16,16,16,16]{3,2,1,0:T(8,128)(2,1)}, s32[]{:T(128)}) %tuple.68), condition=%wide.while_cond.1, body=%wide.while_body.1.sunk | while | flops 2 | bytes 132733 | solution.py:113
  162.2 5.0 reshape.362
  173.8 3.9 collective-permute-start.2
  185.9 7.8 %all-to-all-start.1 = ((bf16[16,2,4,4096]{3,1,2,0:T(2,128)(2,1)}), bf16[16,2,4,4096]{3,1,2,0:T(2,128)(2,1)S(1)}, u32[]{:S(2)}, u32[]{:S(2)}) async-start(bf16[16,2,4,4096]{3,1,2,0:T(2,128)(2,1)} %copy.55), calls=%async_computation.1 | async-start | bytes 2097152 | tf_op jit(solution)/shard_map/all_to_all | solution.py:135
  193.8 31.8 %fusion.18 = f32[4,66,66,258]{3,2,1,0:T(8,128)} fusion(bf16[4,66,1,256]{3,2,1,0:T(2,128)(2,1)} %collective-permute-done.3, bf16[4,66,1,256]{3,2,1,0:T(2,128)(2,1)} %collective-permute-done.2, bf16[4,1,64,256]{3,2,1,0:T(8,128)(2,1)S(1)} %copy-done.4, bf16[4,1,64,256]{3,2,1,0:T(8,128)(2,1)S(1)} %copy-done.2, bf16[3,64,64,256]{3,2,1,0:T(8,128)(2,1)} %get-tuple-element.347, ...), kind=kLoop, calls=%fused_computation.37 | loop fusion | flops 94403232 | bytes 26902656 | tf_op jit(solution)/shard_map/jit(_pad)/pad | solution.py:97
  225.7 19.8 %slice_bitcast_fusion.3 = (f32[66,66,258]{2,1,0:T(8,128)}, f32[66,66,258]{2,1,0:T(8,128)}, f32[66,66,258]{2,1,0:T(8,128)}, f32[66,66,258]{2,1,0:T(8,128)}) fusion(f32[4,66,66,258]{3,2,1,0:T(8,128)} %fusion.18), kind=kLoop, calls=%fused_computation.50 | loop fusion | bytes 35963136 | tf_op jit(solution)/shard_map/squeeze | solution.py:99
  245.5 13.0 %fusion.31 = f32[65,64,256]{2,1,0:T(8,128)} fusion(f32[66,66,258]{2,1,0:T(8,128)} %get-tuple-element.160, f32[66,66,258]{2,1,0:T(8,128)} %get-tuple-element.157), kind=kLoop, calls=%fused_computation.62 | loop fusion | flops 6389760 | bytes 17039360 | tf_op jit(solution)/shard_map/mul | solution.py:38
  258.4 10.7 %fusion.29 = f32[64,65,256]{2,1,0:T(8,128)} fusion(f32[66,66,258]{2,1,0:T(8,128)} %get-tuple-element.160, f32[66,66,258]{2,1,0:T(8,128)} %get-tuple-element.159), kind=kLoop, calls=%fused_computation.58 | loop fusion | flops 6389760 | bytes 17039360 | tf_op jit(solution)/shard_map/mul | solution.py:38
  270.6 5.3 fusion.27
  276.8 134.4 %while.14 = (s32[]{:T(128)}, f32[8,4,3,512]{3,2,1,0:T(4,128)S(1)}, bf16[8,4,3,4096]{3,2,1,0:T(4,128)(2,1)}, f32[8,4,3,512]{3,2,1,0:T(4,128)}, bf16[8,4]{1,0:T(8,...) while((s32[]{:T(128)}, f32[8,4,3,512]{3,2,1,0:T(4,128)S(1)}, ...), condition=%wide.region_3.4_spmd, body=%wide.region_2.3_spmd.sunk | while | flops 134316032 | bytes 582829 | solution.py:63
  278.9 6.2 %fusion.64 = f32[4,4,512]{2,1,0:T(4,128)S(1)} fusion(s32[4,512]{1,0:T(4,128)S(1)} %dynamic-slice_bitcast_fusion.4, bf16[8,4,4,4096]{3,2,1,0:T(4,128)(2,1)S(1)} %get-tuple-element.343, s32[]{:T(128)S(6)} %copy.104), kind=kOutput, calls=%fused_computation.2.clone.1 | convolution fusion | flops 75497472 | bytes 172036 | tf_op jit(solution)/shard_map/while/body/eval_jaxpr/vmap(kc,pc->kp)/dot_general | solution.py:49
  286.0 7.6 %fusion.67 = bf16[8,4,3,4096]{3,2,1,0:T(4,128)(2,1)} fusion(bf16[8,4,3,4096]{3,2,1,0:T(4,128)(2,1)} %get-tuple-element.329, s32[]{:T(128)S(6)} %copy.104, s32[4,512]{1,0:T(4,128)S(1)} %dynamic-slice_bitcast_fusion.4, f32[4,512]{1,0:T(4,128)S(1)} %dynamic-slice_bitcast_fusion.5, f32[4,4,512]{2,1,0:T(4,128)S(1)} %fusion.64, ...), kind=kOutput, calls=%fused_computation.7.clone.1 | convolution fusion | flops 58793984 | bytes 222208 | tf_op jit(solution)/shard_map/while/body/eval_jaxpr/vmap(kp,pc->kc)/dot_general | solution.py:53
  295.7 6.2 %fusion.64 = f32[4,4,512]{2,1,0:T(4,128)S(1)} fusion(s32[4,512]{1,0:T(4,128)S(1)} %dynamic-slice_bitcast_fusion.4, bf16[8,4,4,4096]{3,2,1,0:T(4,128)(2,1)S(1)} %get-tuple-element.343, s32[]{:T(128)S(6)} %copy.104), kind=kOutput, calls=%fused_computation.2.clone.1 | convolution fusion | flops 75497472 | bytes 172036 | tf_op jit(solution)/shard_map/while/body/eval_jaxpr/vmap(kc,pc->kp)/dot_general | solution.py:49
  302.8 7.6 %fusion.67 = bf16[8,4,3,4096]{3,2,1,0:T(4,128)(2,1)} fusion(bf16[8,4,3,4096]{3,2,1,0:T(4,128)(2,1)} %get-tuple-element.329, s32[]{:T(128)S(6)} %copy.104, s32[4,512]{1,0:T(4,128)S(1)} %dynamic-slice_bitcast_fusion.4, f32[4,512]{1,0:T(4,128)S(1)} %dynamic-slice_bitcast_fusion.5, f32[4,4,512]{2,1,0:T(4,128)S(1)} %fusion.64, ...), kind=kOutput, calls=%fused_computation.7.clone.1 | convolution fusion | flops 58793984 | bytes 222208 | tf_op jit(solution)/shard_map/while/body/eval_jaxpr/vmap(kp,pc->kc)/dot_general | solution.py:53
  312.5 6.2 %fusion.64 = f32[4,4,512]{2,1,0:T(4,128)S(1)} fusion(s32[4,512]{1,0:T(4,128)S(1)} %dynamic-slice_bitcast_fusion.4, bf16[8,4,4,4096]{3,2,1,0:T(4,128)(2,1)S(1)} %get-tuple-element.343, s32[]{:T(128)S(6)} %copy.104), kind=kOutput, calls=%fused_computation.2.clone.1 | convolution fusion | flops 75497472 | bytes 172036 | tf_op jit(solution)/shard_map/while/body/eval_jaxpr/vmap(kc,pc->kp)/dot_general | solution.py:49
  319.6 7.6 %fusion.67 = bf16[8,4,3,4096]{3,2,1,0:T(4,128)(2,1)} fusion(bf16[8,4,3,4096]{3,2,1,0:T(4,128)(2,1)} %get-tuple-element.329, s32[]{:T(128)S(6)} %copy.104, s32[4,512]{1,0:T(4,128)S(1)} %dynamic-slice_bitcast_fusion.4, f32[4,512]{1,0:T(4,128)S(1)} %dynamic-slice_bitcast_fusion.5, f32[4,4,512]{2,1,0:T(4,128)S(1)} %fusion.64, ...), kind=kOutput, calls=%fused_computation.7.clone.1 | convolution fusion | flops 58793984 | bytes 222208 | tf_op jit(solution)/shard_map/while/body/eval_jaxpr/vmap(kp,pc->kc)/dot_general | solution.py:53
  329.3 6.2 %fusion.64 = f32[4,4,512]{2,1,0:T(4,128)S(1)} fusion(s32[4,512]{1,0:T(4,128)S(1)} %dynamic-slice_bitcast_fusion.4, bf16[8,4,4,4096]{3,2,1,0:T(4,128)(2,1)S(1)} %get-tuple-element.343, s32[]{:T(128)S(6)} %copy.104), kind=kOutput, calls=%fused_computation.2.clone.1 | convolution fusion | flops 75497472 | bytes 172036 | tf_op jit(solution)/shard_map/while/body/eval_jaxpr/vmap(kc,pc->kp)/dot_general | solution.py:49
  336.4 7.6 %fusion.67 = bf16[8,4,3,4096]{3,2,1,0:T(4,128)(2,1)} fusion(bf16[8,4,3,4096]{3,2,1,0:T(4,128)(2,1)} %get-tuple-element.329, s32[]{:T(128)S(6)} %copy.104, s32[4,512]{1,0:T(4,128)S(1)} %dynamic-slice_bitcast_fusion.4, f32[4,512]{1,0:T(4,128)S(1)} %dynamic-slice_bitcast_fusion.5, f32[4,4,512]{2,1,0:T(4,128)S(1)} %fusion.64, ...), kind=kOutput, calls=%fused_computation.7.clone.1 | convolution fusion | flops 58793984 | bytes 222208 | tf_op jit(solution)/shard_map/while/body/eval_jaxpr/vmap(kp,pc->kc)/dot_general | solution.py:53
  346.1 6.2 %fusion.64 = f32[4,4,512]{2,1,0:T(4,128)S(1)} fusion(s32[4,512]{1,0:T(4,128)S(1)} %dynamic-slice_bitcast_fusion.4, bf16[8,4,4,4096]{3,2,1,0:T(4,128)(2,1)S(1)} %get-tuple-element.343, s32[]{:T(128)S(6)} %copy.104), kind=kOutput, calls=%fused_computation.2.clone.1 | convolution fusion | flops 75497472 | bytes 172036 | tf_op jit(solution)/shard_map/while/body/eval_jaxpr/vmap(kc,pc->kp)/dot_general | solution.py:49
  353.2 7.6 %fusion.67 = bf16[8,4,3,4096]{3,2,1,0:T(4,128)(2,1)} fusion(bf16[8,4,3,4096]{3,2,1,0:T(4,128)(2,1)} %get-tuple-element.329, s32[]{:T(128)S(6)} %copy.104, s32[4,512]{1,0:T(4,128)S(1)} %dynamic-slice_bitcast_fusion.4, f32[4,512]{1,0:T(4,128)S(1)} %dynamic-slice_bitcast_fusion.5, f32[4,4,512]{2,1,0:T(4,128)S(1)} %fusion.64, ...), kind=kOutput, calls=%fused_computation.7.clone.1 | convolution fusion | flops 58793984 | bytes 222208 | tf_op jit(solution)/shard_map/while/body/eval_jaxpr/vmap(kp,pc->kc)/dot_general | solution.py:53
  362.9 6.2 %fusion.64 = f32[4,4,512]{2,1,0:T(4,128)S(1)} fusion(s32[4,512]{1,0:T(4,128)S(1)} %dynamic-slice_bitcast_fusion.4, bf16[8,4,4,4096]{3,2,1,0:T(4,128)(2,1)S(1)} %get-tuple-element.343, s32[]{:T(128)S(6)} %copy.104), kind=kOutput, calls=%fused_computation.2.clone.1 | convolution fusion | flops 75497472 | bytes 172036 | tf_op jit(solution)/shard_map/while/body/eval_jaxpr/vmap(kc,pc->kp)/dot_general | solution.py:49
  370.0 7.6 %fusion.67 = bf16[8,4,3,4096]{3,2,1,0:T(4,128)(2,1)} fusion(bf16[8,4,3,4096]{3,2,1,0:T(4,128)(2,1)} %get-tuple-element.329, s32[]{:T(128)S(6)} %copy.104, s32[4,512]{1,0:T(4,128)S(1)} %dynamic-slice_bitcast_fusion.4, f32[4,512]{1,0:T(4,128)S(1)} %dynamic-slice_bitcast_fusion.5, f32[4,4,512]{2,1,0:T(4,128)S(1)} %fusion.64, ...), kind=kOutput, calls=%fused_computation.7.clone.1 | convolution fusion | flops 58793984 | bytes 222208 | tf_op jit(solution)/shard_map/while/body/eval_jaxpr/vmap(kp,pc->kc)/dot_general | solution.py:53
  379.7 6.2 %fusion.64 = f32[4,4,512]{2,1,0:T(4,128)S(1)} fusion(s32[4,512]{1,0:T(4,128)S(1)} %dynamic-slice_bitcast_fusion.4, bf16[8,4,4,4096]{3,2,1,0:T(4,128)(2,1)S(1)} %get-tuple-element.343, s32[]{:T(128)S(6)} %copy.104), kind=kOutput, calls=%fused_computation.2.clone.1 | convolution fusion | flops 75497472 | bytes 172036 | tf_op jit(solution)/shard_map/while/body/eval_jaxpr/vmap(kc,pc->kp)/dot_general | solution.py:49
  386.8 7.6 %fusion.67 = bf16[8,4,3,4096]{3,2,1,0:T(4,128)(2,1)} fusion(bf16[8,4,3,4096]{3,2,1,0:T(4,128)(2,1)} %get-tuple-element.329, s32[]{:T(128)S(6)} %copy.104, s32[4,512]{1,0:T(4,128)S(1)} %dynamic-slice_bitcast_fusion.4, f32[4,512]{1,0:T(4,128)S(1)} %dynamic-slice_bitcast_fusion.5, f32[4,4,512]{2,1,0:T(4,128)S(1)} %fusion.64, ...), kind=kOutput, calls=%fused_computation.7.clone.1 | convolution fusion | flops 58793984 | bytes 222208 | tf_op jit(solution)/shard_map/while/body/eval_jaxpr/vmap(kp,pc->kc)/dot_general | solution.py:53
  396.5 6.2 %fusion.64 = f32[4,4,512]{2,1,0:T(4,128)S(1)} fusion(s32[4,512]{1,0:T(4,128)S(1)} %dynamic-slice_bitcast_fusion.4, bf16[8,4,4,4096]{3,2,1,0:T(4,128)(2,1)S(1)} %get-tuple-element.343, s32[]{:T(128)S(6)} %copy.104), kind=kOutput, calls=%fused_computation.2.clone.1 | convolution fusion | flops 75497472 | bytes 172036 | tf_op jit(solution)/shard_map/while/body/eval_jaxpr/vmap(kc,pc->kp)/dot_general | solution.py:49
  403.6 7.6 %fusion.67 = bf16[8,4,3,4096]{3,2,1,0:T(4,128)(2,1)} fusion(bf16[8,4,3,4096]{3,2,1,0:T(4,128)(2,1)} %get-tuple-element.329, s32[]{:T(128)S(6)} %copy.104, s32[4,512]{1,0:T(4,128)S(1)} %dynamic-slice_bitcast_fusion.4, f32[4,512]{1,0:T(4,128)S(1)} %dynamic-slice_bitcast_fusion.5, f32[4,4,512]{2,1,0:T(4,128)S(1)} %fusion.64, ...), kind=kOutput, calls=%fused_computation.7.clone.1 | convolution fusion | flops 58793984 | bytes 222208 | tf_op jit(solution)/shard_map/while/body/eval_jaxpr/vmap(kp,pc->kc)/dot_general | solution.py:53
  414.2 7.5 %all-to-all-start.2 = ((bf16[16,2,3,4096]{3,1,2,0:T(2,128)(2,1)}), bf16[16,2,3,4096]{3,1,2,0:T(2,128)(2,1)S(1)}, u32[]{:S(2)}, u32[]{:S(2)}) async-start(bf16[16,2,3,4096]{3,1,2,0:T(2,128)(2,1)} %copy.59), calls=%async_computation.2 | async-start | bytes 1572864 | tf_op jit(solution)/shard_map/all_to_all | solution.py:154
  421.8 13.9 %fusion.34 = f32[64,64,256]{2,1,0:T(8,128)} fusion(f32[64,64,256]{2,1,0:T(8,128)} %param.10, f32[64,64,257]{2,1,0:T(8,128)} %fusion.27, f32[64,65,256]{2,1,0:T(8,128)} %fusion.29, f32[65,64,256]{2,1,0:T(8,128)} %fusion.31), kind=kLoop, calls=%fused_computation.67 | loop fusion | flops 7340032 | bytes 33554432 | tf_op jit(solution)/shard_map/min | solution.py:103
  441.3 34.5 %convolution_bitcast_fusion = f32[3,4,16,4,16,16,16]{6,5,4,2,0,3,1:T(8,128)} fusion(bf16[4,4,16,32,1,1,1]{3,2,6,5,4,1,0:T(8,128)(2,1)S(1)} %bitcast.166, bf16[3,16,16,16,32,1,1]{4,3,2,1,0,6,5:T(8,128)(2,1)S(1)} %bitcast.158), kind=kOutput, calls=%fused_computation.34 | convolution fusion | flops 201326592 | bytes 13385728 | tf_op jit(solution)/shard_map/sb,skc->bkc/dot_general | solution.py:163
  475.8 65.6 %copy.62 = f32[3,4,16,4,16,16,16]{6,5,4,3,2,1,0:T(8,128)} copy(f32[3,4,16,4,16,16,16]{6,5,4,2,0,3,1:T(8,128)} %convolution_bitcast_fusion) | data formatting | bytes 25165824 | tf_op jit(solution)/shard_map/transpose | solution.py:165
  541.4 68.0 %reshape.307 = f32[3,64,64,256]{3,2,1,0:T(8,128)} reshape(f32[3,4,16,4,16,16,16]{6,5,4,3,2,1,0:T(8,128)} %copy.62) | data formatting | bytes 25165824 | tf_op jit(solution)/shard_map/reshape | solution.py:165
  609.4 11.8 %add_convert_fusion = bf16[3,64,64,256]{3,2,1,0:T(8,128)(2,1)} fusion(f32[3,64,64,256]{3,2,1,0:T(8,128)} %reshape.307, bf16[3,64,64,256]{3,2,1,0:T(8,128)(2,1)} %get-tuple-element.347), kind=kLoop, calls=%fused_computation.46 | loop fusion | flops 9437184 | bytes 25165824 | tf_op jit(solution)/shard_map/convert_element_type | solution.py:166
  (218 shorter events, 150.4 us)
Async XLA Ops:
  2.9 183.0 %all-to-all-start = ((bf16[16,1,2]{2,1,0:T(2,128)(2,1)}), bf16[16,1,2]{2,1,0:T(2,128)(2,1)S(1)}, u32[]{:S(2)}, u32[]{:S(2)}) async-start(bf16[16,1,2]{2,1,0:T(2,128)(2,1)} %all_to_all.16), calls=%async_computation | async-start | bytes 16384 | tf_op jit(solution)/shard_map/all_to_all | solution.py:142
  11.2 4.5 copy-start
  15.4 5.9 copy-start.12
  15.4 143.9 %copy-start.9 = (f32[1,1,16,2,512]{4,3,2,1,0:T(2,128)S(1)}, f32[1,1,16,2,512]{4,3,2,1,0:T(2,128)}, u32[]{:S(2)}) copy-start(f32[1,1,16,2,512]{4,3,2,1,0:T(2,128)} %param.15) | copy-start | bytes 196612
  15.4 144.6 %copy-start.10 = (f32[1,1,16,2,512]{4,3,2,1,0:T(2,128)S(1)}, f32[1,1,16,2,512]{4,3,2,1,0:T(2,128)}, u32[]{:S(2)}) copy-start(f32[1,1,16,2,512]{4,3,2,1,0:T(2,128)} %param.16) | copy-start | bytes 196612
  15.4 145.3 %copy-start.11 = (s32[1,1,16,2,512]{4,3,2,1,0:T(2,128)S(1)}, s32[1,1,16,2,512]{4,3,2,1,0:T(2,128)}, u32[]{:S(2)}) copy-start(s32[1,1,16,2,512]{4,3,2,1,0:T(2,128)} %param.17) | copy-start | bytes 196612
  15.4 146.0 %copy-start.8 = (f32[1,1,16,2,3,512]{5,3,4,2,1,0:T(2,128)S(1)}, f32[1,1,16,2,3,512]{5,3,4,2,1,0:T(2,128)}, u32[]{:S(2)}) copy-start(f32[1,1,16,2,3,512]{5,3,4,2,1,0:T(2,128)} %param.14) | copy-start | bytes 589828
  15.7 155.3 %collective-permute-start = (bf16[4,1,64,256]{3,2,1,0:T(8,128)(2,1)S(1)}, bf16[4,1,64,256]{3,2,1,0:T(8,128)(2,1)S(1)}, u32[]{:S(2)}, u32[]{:S(2)}) collective-permute-start(bf16[4,1,64,256]{3,2,1,0:T(8,128)(2,1)S(1)} %get-tuple-element.163), channel_id=1, source_target_pairs={{0,16},{16,32},{32,48},{48,64},{64,80},{80,96},{96,112},{1,17},{17... | collective-permute-start | bytes 393224 | tf_op jit(solution)/shard_map/ppermute | solution.py:20
  17.7 153.4 %collective-permute-start.1 = (bf16[4,1,64,256]{3,2,1,0:T(8,128)(2,1)S(1)}, bf16[4,1,64,256]{3,2,1,0:T(8,128)(2,1)S(1)}, u32[]{:S(2)}, u32[]{:S(2)}) collective-permute-start(bf16[4,1,64,256]{3,2,1,0:T(8,128)(2,1)S(1)} %get-tuple-element.164), channel_id=1, source_target_pairs={{16,0},{32,16},{48,32},{64,48},{80,64},{96,80},{112,96},{17,1},{33... | collective-permute-start | bytes 393224 | tf_op jit(solution)/shard_map/ppermute | solution.py:22
  171.1 9.3 %copy-start.5 = (bf16[16,1,4096]{2,0,1:T(8,128)(2,1)S(1)}, bf16[16,1,4096]{2,0,1:T(8,128)(2,1)}, u32[]{:S(2)}) copy-start(bf16[16,1,4096]{2,0,1:T(8,128)(2,1)} %convert_element_type.63) | copy-start | bytes 393220
  171.1 6.7 %copy-start.1 = (bf16[4,1,64,256]{3,2,1,0:T(8,128)(2,1)}, bf16[4,1,64,256]{3,2,1,0:T(8,128)(2,1)S(1)}, u32[]{:S(2)}) copy-start(bf16[4,1,64,256]{3,2,1,0:T(8,128)(2,1)S(1)} %collective-permute-done) | copy-start | bytes 393220
  171.1 6.7 %copy-start.3 = (bf16[4,1,64,256]{3,2,1,0:T(8,128)(2,1)}, bf16[4,1,64,256]{3,2,1,0:T(8,128)(2,1)S(1)}, u32[]{:S(2)}) copy-start(bf16[4,1,64,256]{3,2,1,0:T(8,128)(2,1)S(1)} %collective-permute-done.1) | copy-start | bytes 393220
  173.8 20.0 %collective-permute-start.2 = (bf16[4,66,1,256]{3,2,1,0:T(2,128)(2,1)}, bf16[4,66,1,256]{3,2,1,0:T(2,128)(2,1)}, u32[]{:S(2)}, u32[]{:S(2)}) collective-permute-start(bf16[4,66,1,256]{3,2,1,0:T(2,128)(2,1)} %get-tuple-element.161), channel_id=1, source_target_pairs={{0,1},{1,2},{2,3},{3,4},{4,5},{5,6},{6,7},{7,8},{8,9},{9,10},{10,1... | collective-permute-start | bytes 405512 | tf_op jit(solution)/shard_map/ppermute | solution.py:20
  177.8 16.0 %collective-permute-start.3 = (bf16[4,66,1,256]{3,2,1,0:T(2,128)(2,1)}, bf16[4,66,1,256]{3,2,1,0:T(2,128)(2,1)}, u32[]{:S(2)}, u32[]{:S(2)}) collective-permute-start(bf16[4,66,1,256]{3,2,1,0:T(2,128)(2,1)} %get-tuple-element.162), channel_id=1, source_target_pairs={{1,0},{2,1},{3,2},{4,3},{5,4},{6,5},{7,6},{8,7},{9,8},{10,9},{11,1... | collective-permute-start | bytes 405512 | tf_op jit(solution)/shard_map/ppermute | solution.py:22
  181.0 12.9 %copy-start.2 = (bf16[4,1,64,256]{3,2,1,0:T(8,128)(2,1)S(1)}, bf16[4,1,64,256]{3,2,1,0:T(8,128)(2,1)}, u32[]{:S(2)}) copy-start(bf16[4,1,64,256]{3,2,1,0:T(8,128)(2,1)} %copy-done.1) | copy-start | bytes 393220
  181.0 12.9 %copy-start.4 = (bf16[4,1,64,256]{3,2,1,0:T(8,128)(2,1)S(1)}, bf16[4,1,64,256]{3,2,1,0:T(8,128)(2,1)}, u32[]{:S(2)}) copy-start(bf16[4,1,64,256]{3,2,1,0:T(8,128)(2,1)} %copy-done.3) | copy-start | bytes 393220
  185.9 90.0 %all-to-all-start.1 = ((bf16[16,2,4,4096]{3,1,2,0:T(2,128)(2,1)}), bf16[16,2,4,4096]{3,1,2,0:T(2,128)(2,1)S(1)}, u32[]{:S(2)}, u32[]{:S(2)}) async-start(bf16[16,2,4,4096]{3,1,2,0:T(2,128)(2,1)} %copy.55), calls=%async_computation.1 | async-start | bytes 2097152 | tf_op jit(solution)/shard_map/all_to_all | solution.py:135
  245.5 23.7 %slice-start.2 = ((s8[7299072]{0:T(1024)(128)(4,1)}), s8[3104768]{0:T(1024)(128)(4,1)S(1)}, s32[]{:S(2)}) async-start(s8[7299072]{0:T(1024)(128)(4,1)} %bitcast.156), calls=%async_computation.5 | async-start | bytes 6209536
  258.4 10.7 %slice-start = ((s8[7299072]{0:T(1024)(128)(4,1)}), s8[4194304]{0:T(1024)(128)(4,1)S(1)}, s32[]{:S(2)}) async-start(s8[7299072]{0:T(1024)(128)(4,1)} %bitcast.154), calls=%async_computation.3 | async-start | bytes 8388608
  258.4 10.7 %slice-start.1 = ((s8[7299072]{0:T(1024)(128)(4,1)}), s8[3104768]{0:T(1024)(128)(4,1)S(1)}, s32[]{:S(2)}) async-start(s8[7299072]{0:T(1024)(128)(4,1)} %bitcast.154), calls=%async_computation.4 | async-start | bytes 6209536
  258.4 12.1 %slice-start.3 = ((s8[7299072]{0:T(1024)(128)(4,1)}), s8[4194304]{0:T(1024)(128)(4,1)S(1)}, s32[]{:S(2)}) async-start(s8[7299072]{0:T(1024)(128)(4,1)} %bitcast.156), calls=%async_computation.6 | async-start | bytes 8388608
  270.6 6.2 copy-start.6
  414.2 22.2 %all-to-all-start.2 = ((bf16[16,2,3,4096]{3,1,2,0:T(2,128)(2,1)}), bf16[16,2,3,4096]{3,1,2,0:T(2,128)(2,1)S(1)}, u32[]{:S(2)}, u32[]{:S(2)}) async-start(bf16[16,2,3,4096]{3,1,2,0:T(2,128)(2,1)} %copy.59), calls=%async_computation.2 | async-start | bytes 1572864 | tf_op jit(solution)/shard_map/all_to_all | solution.py:154
  435.7 5.6 copy-start.7
where the time goes:
time: 633 us; the launch traced here: 621 us
  local copies, waits for them, and re-layouts  337 us (53%)
  matrix products  146 us (23%)
  other arithmetic  102 us (16%)
  starting transfers between devices  35.7 us (6%)
    gather x96, local copies, waits for them, and re-layouts  137 us
    reshape x1, local copies, waits for them, and re-layouts, per_device(): block_field.transpose(3, 0, 4, 1, 5, 2, 6)  68 us
    transpose x1, local copies, waits for them, and re-layouts, per_device(): block_field.transpose(3, 0, 4, 1, 5, 2, 6)  65.6 us
    dot_general x8, matrix products, one_slot(): jnp.einsum('kp,pc->kc', deposit_w, onehot, preferred_element_type=jnp.flo...  60.6 us
    dot_general x8, matrix products, one_slot(): jnp.einsum('kc,pc->kp', block_data, onehot, preferred_element_type=jnp.fl...  49.9 us
    dot_general x1, matrix products, per_device(): jnp.einsum('sb,skc->bkc', placement, returned, preferred_element_type=jnp...  34.5 us
    pad x1, other arithmetic, per_device(): padded = jnp.pad(padded, ((0, 0), (0, 0), (0, 0), (1, 1)))  31.8 us
    mul x3, other arithmetic, face_div(): courant * (jnp.maximum(left_speed, 0.0) * left_frac + jnp.minimum(left_sp...  29 us
  transfers between devices with their start and end apart: 7, of which 0 were waited for; matrix products, arithmetic and copies ran while one was open for 41% of the time, Pallas kernels for 0%

commit v1 on v0

v1 whole, which is shorter than its diff:
```python
import functools

import jax
import jax.numpy as jnp
from jax import lax
from jax.experimental import pallas as pl
from jax.experimental.pallas import tpu as pltpu
from jax.sharding import PartitionSpec as P

CAP = 2
COURANT = 0.025
MESH = pl.DeviceIdType.MESH
F32 = jnp.float32
BF16 = jnp.bfloat16


def corner(block_id, blocks_y, blocks_z):
    first = lax.div(block_id, blocks_y * blocks_z)
    second = lax.rem(lax.div(block_id, blocks_z), blocks_y)
    third = lax.rem(block_id, blocks_z)
    return first, second, third


def cell_parts(cell):
    row = jnp.floor(cell * (1.0 / 16.0))
    return row, cell - 16.0 * row


def hot_rows(row):
    parcels = row.shape[-1]
    ids = lax.broadcasted_iota(jnp.int32, (256, parcels), 0).astype(F32)
    return jnp.where(ids == row, 1.0, 0.0).astype(BF16)


def hot_depth(depth):
    parcels = depth.shape[-1]
    ids = lax.broadcasted_iota(jnp.int32, (16, parcels), 0).astype(F32)
    return jnp.where(ids == depth, 1.0, 0.0)


def exchange_kernel(
    groups,
    members,
    block_hbm,
    owner_hbm,
    vel_hbm,
    frac_hbm,
    pv_hbm,
    pr_hbm,
    pw_hbm,
    pc_hbm,
    vel_v,
    next_v,
    source_ref,
    back_ref,
    frac_v,
    pv_v,
    pr_v,
    pw_v,
    pc_v,
    pack_v,
    got_v,
    block_v,
    samp_v,
    give_v,
    fluxx_v,
    hxu_v,
    hxf_v,
    hxn_v,
    hyu_v,
    hyf_v,
    hyn_v,
    syu_v,
    syf_v,
    syn_v,
    block_s,
    owner_s,
    place_s,
    slot_s,
    name_sem,
    parcel_sem,
    load_sem,
    send_sem,
    recv_sem,
    back_send,
    back_recv,
    face_send,
    face_recv,
):
    group = lax.axis_index("group")
    member = lax.axis_index("member")
    drops = owner_hbm.shape[0]
    blocks_x, _, blocks_y, _, depth = frac_hbm.shape
    parcels = pv_hbm.shape[-1]
    blocks_z = depth // 16

    parcel_loads = [
        pltpu.make_async_copy(src, dst, parcel_sem.at[i])
        for i, (src, dst) in enumerate(
            [(pv_hbm, pv_v), (pr_hbm, pr_v), (pw_hbm, pw_v), (pc_hbm, pc_v)]
        )
    ]
    loads = []
    for c in range(blocks_x):
        loads.append(
            (
                pltpu.make_async_copy(frac_hbm.at[c], frac_v.at[c], load_sem.at[0, c]),
                pltpu.make_async_copy(vel_hbm.at[:, c], vel_v.at[:, c], load_sem.at[1, c]),
            )
        )
    names = [
        pltpu.make_async_copy(block_hbm, block_s, name_sem.at[0]),
        pltpu.make_async_copy(owner_hbm, owner_s, name_sem.at[1]),
    ]
    for copy in names + parcel_loads:
        copy.start()
    for pair in loads:
        for copy in pair:
            copy.start()

    up = lax.rem(group + 1, groups)
    down = lax.rem(group + groups - 1, groups)
    right = lax.rem(member + 1, members)
    left = lax.rem(member + members - 1, members)
    barrier = pltpu.get_barrier_semaphore()
    for i in range(1, members):
        peer = lax.rem(member + i, members)
        pl.semaphore_signal(barrier, inc=1, device_id=(group, peer), device_id_type=MESH)
    for near in (up, down):
        pl.semaphore_signal(barrier, inc=1, device_id=(near, member), device_id_type=MESH)

    for copy in names:
        copy.wait()
    owners = [owner_s[j] for j in range(drops)]
    slots = []
    for j in range(drops):
        place = jnp.int32(0)
        for i in range(j):
            place = place + jnp.where(owners[i] == owners[j], 1, 0)
        place_s[j] = place
        slots.append(owners[j] * CAP + place)
    for s in range(members * CAP):
        found = jnp.int32(drops)
        for j in range(drops):
            found = jnp.where(slots[j] == s, j, found)
        slot_s[s] = found

    for copy in parcel_loads:
        copy.wait()
    pack_v[:, 0:3] = pv_v[...]
    pack_v[:, 3] = pr_v[...] * pw_v[...]
    pack_v[:, 4] = pc_v[...].astype(F32)

    pl.semaphore_wait(barrier, members + 1)

    sends = []
    for i in range(1, members):
        peer = lax.rem(member + i, members)
        copy = pltpu.make_async_remote_copy(
            src_ref=pack_v.at[peer],
            dst_ref=got_v.at[member],
            send_sem=send_sem.at[i],
            recv_sem=recv_sem.at[i],
            device_id=(group, peer),
            device_id_type=MESH,
        )
        copy.start()
        sends.append(copy)
    got_v[member] = pack_v[member]

    def face(src, dst, number, device):
        copy = pltpu.make_async_remote_copy(
            src_ref=src,
            dst_ref=dst,
            send_sem=face_send.at[number],
            recv_sem=face_recv.at[number],
            device_id=device,
            device_id_type=MESH,
        )
        copy.start()
        return copy

    faces = [
        face(vel_hbm.at[0, blocks_x - 1, 15], hxu_v, 0, (up, member)),
        face(frac_hbm.at[blocks_x - 1, 15], hxf_v, 1, (up, member)),
        face(frac_hbm.at[0, 0], hxn_v, 2, (down, member)),
    ]

    for c in range(blocks_x):
        for copy in loads[c]:
            copy.wait()

        def edge(x, carry):
            syf_v[c, x] = frac_v[c, x, blocks_y - 1, 15:16, :]
            syn_v[c, x] = frac_v[c, x, 0, 0:1, :]
            syu_v[c, x] = vel_v[1, c, x, blocks_y - 1].astype(F32)[15:16]
            return carry

        lax.fori_loop(0, 16, edge, 0, unroll=8)
    faces += [
        face(syu_v, hyu_v, 3, (group, right)),
        face(syf_v, hyf_v, 4, (group, right)),
        face(syn_v, hyn_v, 5, (group, left)),
    ]

    column = lax.broadcasted_iota(jnp.int32, (64, depth), 0)
    lane = lax.broadcasted_iota(jnp.int32, (64, depth), 1)

    def extract(j, carry):
        bx, by, bz = corner(block_s[j], blocks_y, blocks_z)
        wanted = lane - bz * 16
        total = jnp.zeros((64, 256), F32)
        for k in range(4):
            if k < 3:
                part = vel_v[k, bx, :, by]
            else:
                part = frac_v[bx, :, by].astype(BF16)
            part = part.reshape(256, depth)
            pick = jnp.where(wanted == column - 16 * k, 1.0, 0.0)
            pick = jnp.where(column // 16 == k, pick, 0.0).astype(BF16)
            total = total + lax.dot_general(
                pick, part, (((1,), (1,)), ((), ())), preferred_element_type=F32
            )
        block_v[j] = total.astype(BF16)
        return carry

    lax.fori_loop(0, drops, extract, 0, unroll=4)

    for i in range(1, members):
        peer = lax.rem(member + members - i, members)
        pltpu.make_async_remote_copy(
            src_ref=pack_v.at[peer],
            dst_ref=got_v.at[peer],
            send_sem=send_sem.at[i],
            recv_sem=recv_sem.at[i],
            device_id=(group, peer),
            device_id_type=MESH,
        ).wait_recv()

    def pair_row(j, q):
        both = got_v[owner_s[j], q]
        return jnp.where(place_s[j] == 0, both[0:1], both[1:2])

    def sample(j, carry):
        row, deep = cell_parts(pair_row(j, 4))
        picked = jnp.dot(block_v[j], hot_rows(row), preferred_element_type=F32)
        hot = hot_depth(deep)
        for q in range(4):
            samp_v[j, q : q + 1] = jnp.sum(
                picked[16 * q : 16 * q + 16] * hot, axis=0, keepdims=True
            )
        return carry

    lax.fori_loop(0, drops, sample, 0, unroll=4)
    samp_v[drops, 0:3] = jnp.zeros((3, parcels), F32)
    samp_v[drops, 3:4] = jnp.ones((1, parcels), F32)

    def give(s, carry):
        give_v[s // CAP, s % CAP] = samp_v[slot_s[s]].astype(BF16)
        return carry

    lax.fori_loop(0, members * CAP, give, 0, unroll=8)
    for i in range(1, members):
        peer = lax.rem(member + i, members)
        copy = pltpu.make_async_remote_copy(
            src_ref=give_v.at[peer],
            dst_ref=back_ref.at[member],
            send_sem=back_send.at[i],
            recv_sem=back_recv.at[i],
            device_id=(group, peer),
            device_id_type=MESH,
        )
        copy.start()
        sends.append(copy)
    back_ref[member] = give_v[member]

    def scatter(j, carry):
        row, deep = cell_parts(pair_row(j, 4))
        hot = hot_depth(deep)
        pull = pair_row(j, 3) * (1.0 - samp_v[j, 3:4])
        parts = []
        for q in range(3):
            drag = pull * (samp_v[j, q : q + 1] - pair_row(j, q))
            parts.append((drag.astype(BF16).astype(F32) * hot).astype(BF16))
        spread = jnp.concatenate(parts, axis=0)
        source = lax.dot_general(
            hot_rows(row), spread, (((1,), (1,)), ((), ())), preferred_element_type=F32
        )
        source_ref[j] = source.astype(BF16)
        return carry

    lax.fori_loop(0, drops, scatter, 0, unroll=4)

    for copy in faces:
        copy.wait()
    low_x = jnp.where(group > 0, 1.0, 0.0)
    high_x = jnp.where(group < groups - 1, 1.0, 0.0)
    low_y = jnp.where(member > 0, 1.0, 0.0)
    high_y = jnp.where(member < members - 1, 1.0, 0.0)
    frac_v[blocks_x, 0] = hxn_v[...] * high_x

    def flux(speed, here, there):
        return speed * jnp.where(speed > 0.0, here, there)

    fluxx_v[...] = flux(hxu_v[...].astype(F32) * low_x, hxf_v[...], frac_v[0, 0])

    def full(row):
        return jnp.broadcast_to(row, (8, 128))

    row_id = lax.broadcasted_iota(jnp.int32, (8, 128), 0)
    lane_id = lax.broadcasted_iota(jnp.int32, (8, 128), 1)
    first_row, last_row = row_id == 0, row_id == 7
    first_lane, last_lane = lane_id == 0, lane_id == 127
    halves = [slice(h * 128, h * 128 + 128) for h in range(depth // 128)]
    tiles = blocks_y * 2

    def split(row):
        return [full(row[:, h]) for h in halves]

    def one_plane(bx, x):
        def at(t):
            return t // 2, slice(8 * (t % 2), 8 * (t % 2) + 8)

        def speeds(k, t):
            pairs = [vel_v[k, bx, x, t, :, h].astype(F32) for h in halves]
            return [[p[8 * i : 8 * i + 8] for p in pairs] for i in range(2)]

        after = bx * 16 + x + 1
        bn, xn = lax.div(after, 16), lax.rem(after, 16)
        here = [[frac_v[(bx, x) + at(t) + (h,)] for h in halves] for t in range(tiles)]
        behind = split(flux(hyu_v[bx, x] * low_y, hyf_v[bx, x], frac_v[bx, x, 0, 0:1, :]))
        beyond = split(hyn_v[bx, x] * high_y)
        rolled = [pltpu.roll(f, 7, 0) for f in here[0]]
        for t in range(tiles):
            if t % 2 == 0:
                pair = [speeds(k, t // 2) for k in range(3)]
            speed = [pair[k][t % 2] for k in range(3)]
            if t + 1 < tiles:
                rolled_next = [pltpu.roll(f, 7, 0) for f in here[t + 1]]
            else:
                rolled_next = beyond
            lanes = [pltpu.roll(f, 127, 1) for f in here[t]] + [jnp.zeros((8, 128), F32)]
            deep = [
                flux(speed[2][i], here[t][i], jnp.where(last_lane, lanes[i + 1], lanes[i]))
                for i in range(len(halves))
            ]
            turned = [jnp.zeros((8, 128), F32)] + [pltpu.roll(d, 1, 1) for d in deep]
            for i, h in enumerate(halves):
                spot = at(t) + (h,)
                now = flux(speed[0][i], here[t][i], frac_v[(bn, xn) + spot])
                change = now - fluxx_v[spot]
                fluxx_v[spot] = now
                ahead = jnp.where(last_row, rolled_next[i], rolled[i])
                now = flux(speed[1][i], here[t][i], ahead)
                moved = pltpu.roll(now, 1, 0)
                change = change + (now - jnp.where(first_row, behind[i], moved))
                behind[i] = moved
                under = jnp.where(first_lane, turned[i], turned[i + 1])
                change = change + (deep[i] - under)
                next_v[(bx, x) + spot] = jnp.minimum(here[t][i] - COURANT * change, 1.0)
            rolled = rolled_next

    def plane(n, carry):
        bx, x = lax.div(n, 4), lax.rem(n, 4) * 4
        for i in range(4):
            one_plane(bx, x + i)
        return carry

    lax.fori_loop(0, blocks_x * 4, plane, 0)

    for i in range(1, members):
        peer = lax.rem(member + members - i, members)
        pltpu.make_async_remote_copy(
            src_ref=give_v.at[peer],
            dst_ref=back_ref.at[peer],
            send_sem=back_send.at[i],
            recv_sem=back_recv.at[i],
            device_id=(group, peer),
            device_id_type=MESH,
        ).wait_recv()
    for copy in sends:
        copy.wait_send()


def field_kernel(
    block_s,
    vel_ref,
    next_ref,
    source_ref,
    back_ref,
    pv_ref,
    pr_ref,
    frac_out,
    vel_out,
    pv_out,
    fresh_v,
    lead_s,
    store_sem,
    block_sem,
):
    drops = block_s.shape[0]
    members = back_ref.shape[0]
    _, blocks_x, _, blocks_y, _, depth = vel_ref.shape
    blocks_z = depth // 16
    bulk = [
        pltpu.make_async_copy(vel_ref.at[:, c], vel_out.at[:, c], store_sem.at[c])
        for c in range(blocks_x)
    ]
    frac_copy = pltpu.make_async_copy(next_ref, frac_out, store_sem.at[blocks_x])
    for copy in bulk + [frac_copy]:
        copy.start()

    keys = [lax.div(block_s[j], 8) for j in range(drops)]
    for j in range(drops):
        lead = jnp.int32(j)
        for i in reversed(range(j)):
            lead = jnp.where(keys[i] == keys[j], i, lead)
        lead_s[j] = lead

    def spot(j):
        bx, by, bz = corner(block_s[j], blocks_y, blocks_z)
        z0 = pl.multiple_of(lax.div(bz, 8) * 128, 128)
        return bx, by, pl.ds(z0, 128), lax.rem(bz, 8) * 16

    def begin(j, carry):
        bx, by, lanes, _ = spot(j)
        for k in range(3):
            fresh_v[j, k] = vel_ref[k, bx, :, by, :, lanes]
        return carry

    lax.fori_loop(0, drops, begin, 0, unroll=4)

    lane = lax.broadcasted_iota(jnp.int32, (48, 128), 1)
    column = lax.broadcasted_iota(jnp.int32, (48, 128), 0)

    def patch(j, carry):
        _, _, _, shift = spot(j)
        wanted = lane - shift
        source = source_ref[j]
        lead = lead_s[j]
        for k in range(3):
            pick = jnp.where(wanted == column - 16 * k, 1.0, 0.0)
            pick = jnp.where(column // 16 == k, pick, 0.0).astype(BF16)
            moved = jnp.dot(source, pick, preferred_element_type=F32)
            old = fresh_v[lead, k].astype(F32).reshape(256, 128)
            fresh_v[lead, k] = (old + moved).astype(BF16).reshape(16, 16, 128)
        return carry

    lax.fori_loop(0, drops, patch, 0, unroll=4)

    def block_copy(j):
        bx, by, lanes, _ = spot(j)
        return pltpu.make_async_copy(
            fresh_v.at[j], vel_out.at[:, bx, :, by, :, lanes], block_sem.at[j]
        )

    for copy in bulk:
        copy.wait()
    for j in range(drops):

        @pl.when(lead_s[j] == j)
        def _():
            block_copy(j).start()

    def gain_pair(owner, carry):
        sampled = [back_ref[owner, place].astype(F32) for place in range(CAP)]
        rate = pr_ref[owner]
        old = pv_ref[owner]
        share = jnp.concatenate([s[3:4] for s in sampled], axis=0)
        pull = rate * (1.0 - share)
        for q in range(3):
            speed = jnp.concatenate([s[q : q + 1] for s in sampled], axis=0)
            pv_out[owner, q] = old[q] + pull * (speed - old[q])
        return carry

    lax.fori_loop(0, members, gain_pair, 0, unroll=4)
    frac_copy.wait()
    for j in range(drops):

        @pl.when(lead_s[j] == j)
        def _():
            block_copy(j).wait()


def solution(mesh):
    groups, members = mesh.shape["group"], mesh.shape["member"]

    def per_device(
        volume_frac,
        velocity,
        drop_block,
        drop_owner,
        parcel_vel,
        parcel_rate,
        parcel_weight,
        parcel_cell,
    ):
        planes, rows, depth = volume_frac.shape
        parcels = parcel_vel.shape[-1]
        drops = drop_block.shape[-1]
        block_ids = drop_block.reshape(drops)
        owners = drop_owner.reshape(drops)
        pv = parcel_vel[0, 0].transpose(0, 2, 1, 3)
        pr, pw, pc = parcel_rate[0, 0], parcel_weight[0, 0], parcel_cell[0, 0]
        smem = pl.BlockSpec(memory_space=pltpu.SMEM)
        vmem = pl.BlockSpec(memory_space=pltpu.VMEM)
        hbm = pl.BlockSpec(memory_space=pltpu.HBM)
        shaped = jax.ShapeDtypeStruct
        blocks_x, blocks_y = planes // 16, rows // 16
        vel6 = velocity.reshape(3, blocks_x, 16, blocks_y, 16, depth)
        frac5 = volume_frac.reshape(blocks_x, 16, blocks_y, 16, depth)
        face_x = (blocks_y, 16, depth)
        face_y = (blocks_x, 16, 1, depth)
        inputs = [
            pltpu.with_memory_space_constraint(a, pltpu.HBM)
            for a in (block_ids, owners, vel6, frac5, pv, pr, pw, pc)
        ]
        vel_now, frac_next, source, back = pl.pallas_call(
            functools.partial(exchange_kernel, groups, members),
            out_shape=(
                shaped(vel6.shape, BF16),
                shaped(frac5.shape, F32),
                shaped((drops, 256, 48), BF16),
                shaped((members, CAP, 4, parcels), BF16),
            ),
            in_specs=[hbm] * 8,
            out_specs=(vmem,) * 4,
            scratch_shapes=[
                pltpu.VMEM((blocks_x + 1, 16, blocks_y, 16, depth), F32),
                pltpu.VMEM(pv.shape, F32),
                pltpu.VMEM(pr.shape, F32),
                pltpu.VMEM(pw.shape, F32),
                pltpu.VMEM(pc.shape, jnp.int32),
                pltpu.VMEM((members, 5, CAP, parcels), F32),
                pltpu.VMEM((members, 5, CAP, parcels), F32),
                pltpu.VMEM((drops, 64, 256), BF16),
                pltpu.VMEM((drops + 1, 4, parcels), F32),
                pltpu.VMEM((members, CAP, 4, parcels), BF16),
                pltpu.VMEM(face_x, F32),
                pltpu.VMEM(face_x, BF16),
                pltpu.VMEM(face_x, F32),
                pltpu.VMEM(face_x, F32),
                pltpu.VMEM(face_y, F32),
                pltpu.VMEM(face_y, F32),
                pltpu.VMEM(face_y, F32),
                pltpu.VMEM(face_y, F32),
                pltpu.VMEM(face_y, F32),
                pltpu.VMEM(face_y, F32),
                pltpu.SMEM((drops,), jnp.int32),
                pltpu.SMEM((drops,), jnp.int32),
                pltpu.SMEM((drops,), jnp.int32),
                pltpu.SMEM((members * CAP,), jnp.int32),
                pltpu.SemaphoreType.DMA((2,)),
                pltpu.SemaphoreType.DMA((4,)),
                pltpu.SemaphoreType.DMA((2, blocks_x)),
                pltpu.SemaphoreType.DMA((members,)),
                pltpu.SemaphoreType.DMA((members,)),
                pltpu.SemaphoreType.DMA((members,)),
                pltpu.SemaphoreType.DMA((members,)),
                pltpu.SemaphoreType.DMA((6,)),
                pltpu.SemaphoreType.DMA((6,)),
            ],
            compiler_params=pltpu.CompilerParams(
                collective_id=0, has_side_effects=True, vmem_limit_bytes=40 << 20
            ),
            name="exchange",
        )(*inputs)
        frac_next, velocity_next, pv_next = pl.pallas_call(
            field_kernel,
            out_shape=(
                shaped(frac5.shape, F32),
                shaped(vel6.shape, BF16),
                shaped(pv.shape, F32),
            ),
            in_specs=[smem] + [vmem] * 6,
            out_specs=(hbm, hbm, vmem),
            scratch_shapes=[
                pltpu.VMEM((drops, 3, 16, 16, 128), BF16),
                pltpu.SMEM((drops,), jnp.int32),
                pltpu.SemaphoreType.DMA((blocks_x + 1,)),
                pltpu.SemaphoreType.DMA((drops,)),
            ],
            compiler_params=pltpu.CompilerParams(vmem_limit_bytes=40 << 20),
            name="field",
        )(block_ids, vel_now, frac_next, source, back, pv, pr)
        frac_next = frac_next.reshape(volume_frac.shape)
        velocity_next = velocity_next.reshape(velocity.shape)
        parcel_next = pv_next.transpose(0, 2, 1, 3)[None, None]
        return frac_next, velocity_next, parcel_next

    return jax.shard_map(
        per_device,
        mesh=mesh,
        in_specs=(
            P("group", "member", None),
            P(None, "group", "member", None),
            P("group", "member", None),
            P("group", "member", None, None),
            P("group", "member", None, None, None, None),
            P("group", "member", None, None, None),
            P("group", "member", None, None, None),
            P("group", "member", None, None, None),
        ),
        out_specs=(
            P("group", "member", None),
            P(None, "group", "member", None),
            P("group", "member", None, None, None, None),
        ),
        check_vma=False,
    )
```

time: 633 us -> 30.6 us (0.05)
  the two profiles are of different devices: /device:TPU:26 before, /device:TPU:0 now
where the time goes in v1:
time: 30.6 us; the launch traced here: 30.2 us
  Pallas kernels  29.5 us (96%)
  between operations  0.69 us (2%)
    pallas_call x1, Pallas kernels, per_device(): pl.pallas_call(functools.partial(exchange_kernel, groups, members), out_s...  23.5 us
    pallas_call x1, Pallas kernels, per_device(): pl.pallas_call(field_kernel, out_shape=(shaped(frac5.shape, F32), shaped(...  6.02 us

profile of v1, /device:TPU:0, one launch (start us, length us, event | category | flops | bytes accessed | tf_op | source)
XLA Modules:
  0.0 30.2 jit_solution(247359290240177061)
XLA Ops:
  0.6 0.0 copy-start.1
  0.6 0.0 copy-start
  0.7 0.0 copy-start.2
  0.7 23.5 %exchange.1 = (bf16[3,4,16,4,16,256]{5,4,3,2,1,0:T(8,128)(2,1)S(1)}, f32[4,16,4,16,256]{4,3,2,1,0:T(8,128)S(1)}, bf16[16,256,48]{2,1,0:T(8,128)(2,1)S(1)}, bf16[16,2,4,512]{3,2,1,0:T(4,128)(2,1)S(1)}) custom-call(s32[16]{0:T(128)} %bitcast.19, s32[16]{0:T(128)} %bitcast.25, bf16[3,4,16,4,16,256]{5,4,3,2,1,0:T(8,128)(2,1)} %bitcast.21, ...), custom_call_target="tpu_custom_call" | custom-call | tf_op jit(solution)/shard_map/exchange/pallas_call | solution.py:518
  24.2 0.0 copy-done.1
  24.2 0.0 copy-done
  24.2 0.0 copy-done.2
  24.2 6.0 %field.1 = (f32[4,16,4,16,256]{4,3,2,1,0:T(8,128)}, bf16[3,4,16,4,16,256]{5,4,3,2,1,0:T(8,128)(2,1)}, f32[16,3,2,512]{3,2,1,0:T(2,128)}) custom-call(s32[16]{0:T(128)S(1)} %bitcast.20, bf16[3,4,16,4,16,256]{5,4,3,2,1,0:T(8,128)(2,1)S(1)} %get-tuple-element.10.vel_ref, f32[4,16,4,16,256]{4,3,2,1,0:T(8,128)S(1)} %get-tuple-element.11.next_ref, ...), custom_call_target="tpu_custom_call" | custom-call | tf_op jit(solution)/shard_map/field/pallas_call | solution.py:568
Async XLA Ops:
  0.6 23.5 %copy-start.1 = (f32[1,1,16,2,512]{4,3,2,1,0:T(2,128)S(1)}, f32[1,1,16,2,512]{4,3,2,1,0:T(2,128)}, u32[]{:S(2)}) copy-start(f32[1,1,16,2,512]{4,3,2,1,0:T(2,128)} %param.13) | copy-start | bytes 196612
  0.6 23.5 %copy-start = (f32[1,1,16,2,3,512]{5,3,4,2,1,0:T(2,128)S(1)}, f32[1,1,16,2,3,512]{5,3,4,2,1,0:T(2,128)}, u32[]{:S(2)}) copy-start(f32[1,1,16,2,3,512]{5,3,4,2,1,0:T(2,128)} %param.12) | copy-start | bytes 589828
  0.7 23.5 %copy-start.2 = (s32[1,1,16]{2,1,0:T(1,128)S(1)}, s32[1,1,16]{2,1,0:T(1,128)}, u32[]{:S(2)}) copy-start(s32[1,1,16]{2,1,0:T(1,128)} %param.10) | copy-start | bytes 196

commit v2 on v1

--- a/solution.py
+++ b/solution.py
@@ -100,22 +100,20 @@
             [(pv_hbm, pv_v), (pr_hbm, pr_v), (pw_hbm, pw_v), (pc_hbm, pc_v)]
         )
     ]
-    loads = []
-    for c in range(blocks_x):
-        loads.append(
-            (
-                pltpu.make_async_copy(frac_hbm.at[c], frac_v.at[c], load_sem.at[0, c]),
-                pltpu.make_async_copy(vel_hbm.at[:, c], vel_v.at[:, c], load_sem.at[1, c]),
-            )
+    def chunk_loads(c):
+        return (
+            pltpu.make_async_copy(frac_hbm.at[c], frac_v.at[c], load_sem.at[0, c]),
+            pltpu.make_async_copy(vel_hbm.at[:, c], vel_v.at[:, c], load_sem.at[1, c]),
         )
+
     names = [
         pltpu.make_async_copy(block_hbm, block_s, name_sem.at[0]),
         pltpu.make_async_copy(owner_hbm, owner_s, name_sem.at[1]),
     ]
     for copy in names + parcel_loads:
         copy.start()
-    for pair in loads:
-        for copy in pair:
+    for c in range(blocks_x):
+        for copy in chunk_loads(c):
             copy.start()
 
     up = lax.rem(group + 1, groups)
@@ -151,6 +149,99 @@
     pack_v[:, 3] = pr_v[...] * pw_v[...]
     pack_v[:, 4] = pc_v[...].astype(F32)
 
+    low_x = jnp.where(group > 0, 1.0, 0.0)
+    high_x = jnp.where(group < groups - 1, 1.0, 0.0)
+    low_y = jnp.where(member > 0, 1.0, 0.0)
+    high_y = jnp.where(member < members - 1, 1.0, 0.0)
+
+    def flux(speed, here, there):
+        return speed * jnp.where(speed > 0.0, here, there)
+
+    row_id = lax.broadcasted_iota(jnp.int32, (8, 128), 0)
+    lane_id = lax.broadcasted_iota(jnp.int32, (8, 128), 1)
+    first_row, last_row = row_id == 0, row_id == 7
+    first_lane, last_lane = lane_id == 0, lane_id == 127
+    halves = [slice(h * 128, h * 128 + 128) for h in range(depth // 128)]
+    tiles = blocks_y * 2
+    nothing = jnp.zeros((8, 128), F32)
+
+    def one_plane(bx, x):
+        def at(t):
+            return t // 2, slice(8 * (t % 2), 8 * (t % 2) + 8)
+
+        def speeds(k, t):
+            pairs = [vel_v[k, bx, x, t, :, h].astype(F32) for h in halves]
+            return [[p[8 * i : 8 * i + 8] for p in pairs] for i in range(2)]
+
+        after = bx * 16 + x + 1
+        bn, xn = lax.div(after, 16), lax.rem(after, 16)
+        here = [[frac_v[(bx, x) + at(t) + (h,)] for h in halves] for t in range(tiles)]
+        behind = [nothing] * len(halves)
+        rolled = [pltpu.roll(f, 7, 0) for f in here[0]]
+        for t in range(tiles):
+            if t % 2 == 0:
+                pair = [speeds(k, t // 2) for k in range(3)]
+            speed = [pair[k][t % 2] for k in range(3)]
+            if t + 1 < tiles:
+                rolled_next = [pltpu.roll(f, 7, 0) for f in here[t + 1]]
+            else:
+                rolled_next = [nothing] * len(halves)
+            lanes = [pltpu.roll(f, 127, 1) for f in here[t]] + [nothing]
+            deep = [
+                flux(speed[2][i], here[t][i], jnp.where(last_lane, lanes[i + 1], lanes[i]))
+                for i in range(len(halves))
+            ]
+            turned = [nothing] + [pltpu.roll(d, 1, 1) for d in deep]
+            for i, h in enumerate(halves):
+                spot = at(t) + (h,)
+                now = flux(speed[0][i], here[t][i], frac_v[(bn, xn) + spot])
+                change = now - fluxx_v[spot]
+                fluxx_v[spot] = now
+                ahead = jnp.where(last_row, rolled_next[i], rolled[i])
+                now = flux(speed[1][i], here[t][i], ahead)
+                moved = pltpu.roll(now, 1, 0)
+                change = change + (now - jnp.where(first_row, behind[i], moved))
+                behind[i] = moved
+                under = jnp.where(first_lane, turned[i], turned[i + 1])
+                change = change + (deep[i] - under)
+                fresh = here[t][i] - COURANT * change
+                capped = jnp.minimum(fresh, 1.0)
+                if t == 0:
+                    capped = jnp.where(first_row, fresh, capped)
+                if t == tiles - 1:
+                    capped = jnp.where(last_row, fresh, capped)
+                next_v[(bx, x) + spot] = capped
+            rolled = rolled_next
+
+    quads = blocks_x * 4
+
+    def quad(n):
+        bx, x = lax.div(n, 4), lax.rem(n, 4) * 4
+        for i in range(4):
+            one_plane(bx, x + i)
+
+    def mend(n, carry):
+        bx, x = lax.div(n, 16), lax.rem(n, 16)
+        gain = flux(hyu_v[bx, x] * low_y, hyf_v[bx, x], syn_v[bx, x])
+        old = next_v[bx, x, 0, 0:1, :]
+        next_v[bx, x, 0, 0:1, :] = jnp.minimum(old + COURANT * gain, 1.0)
+        loss = jnp.minimum(syu_v[bx, x], 0.0) * (hyn_v[bx, x] * high_y)
+        old = next_v[bx, x, blocks_y - 1, 15:16, :]
+        next_v[bx, x, blocks_y - 1, 15:16, :] = jnp.minimum(old - COURANT * loss, 1.0)
+        return carry
+
+    def edges(c):
+        for copy in chunk_loads(c):
+            copy.wait()
+
+        def edge(x, carry):
+            syf_v[c, x] = frac_v[c, x, blocks_y - 1, 15:16, :]
+            syn_v[c, x] = frac_v[c, x, 0, 0:1, :]
+            syu_v[c, x] = vel_v[1, c, x, blocks_y - 1].astype(F32)[15:16]
+            return carry
+
+        lax.fori_loop(0, 16, edge, 0, unroll=8)
+
     pl.semaphore_wait(barrier, members + 1)
 
     sends = []
@@ -177,7 +268,6 @@
             device_id=device,
             device_id_type=MESH,
         )
-        copy.start()
         return copy
 
     faces = [
@@ -185,188 +275,138 @@
         face(frac_hbm.at[blocks_x - 1, 15], hxf_v, 1, (up, member)),
         face(frac_hbm.at[0, 0], hxn_v, 2, (down, member)),
     ]
-
-    for c in range(blocks_x):
-        for copy in loads[c]:
-            copy.wait()
-
-        def edge(x, carry):
-            syf_v[c, x] = frac_v[c, x, blocks_y - 1, 15:16, :]
-            syn_v[c, x] = frac_v[c, x, 0, 0:1, :]
-            syu_v[c, x] = vel_v[1, c, x, blocks_y - 1].astype(F32)[15:16]
+    for copy in faces:
+        copy.start()
+
+    def side_faces():
+        return [
+            face(syu_v, hyu_v, 3, (group, right)),
+            face(syf_v, hyf_v, 4, (group, right)),
+            face(syn_v, hyn_v, 5, (group, left)),
+        ]
+
+    def drag():
+        column = lax.broadcasted_iota(jnp.int32, (64, 128), 0)
+        lane = lax.broadcasted_iota(jnp.int32, (64, 128), 1)
+
+        def extract(j, carry):
+            bx, by, bz = corner(block_s[j], blocks_y, blocks_z)
+            half = lax.div(bz, 8)
+            wanted = lane - lax.rem(bz, 8) * 16
+            total = jnp.zeros((64, 256), F32)
+            for k in range(4):
+                if k < 3:
+                    part = vel_v[k, bx, :, by]
+                else:
+                    part = frac_v[bx, :, by].astype(BF16)
+                part = part.reshape(256, depth)
+                for h in range(1, depth // 128):
+                    keep = part[:, :128] if h == 1 else keep
+                    keep = jnp.where(half == h, part[:, 128 * h : 128 * h + 128], keep)
+                part = keep if depth > 128 else part
+                pick = jnp.where(wanted == column - 16 * k, 1.0, 0.0)
+                pick = jnp.where(column // 16 == k, pick, 0.0).astype(BF16)
+                total = total + lax.dot_general(
+                    pick, part, (((1,), (1,)), ((), ())), preferred_element_type=F32
+                )
+            block_v[j] = total.astype(BF16)
             return carry
 
-        lax.fori_loop(0, 16, edge, 0, unroll=8)
-    faces += [
-        face(syu_v, hyu_v, 3, (group, right)),
-        face(syf_v, hyf_v, 4, (group, right)),
-        face(syn_v, hyn_v, 5, (group, left)),
-    ]
-
-    column = lax.broadcasted_iota(jnp.int32, (64, depth), 0)
-    lane = lax.broadcasted_iota(jnp.int32, (64, depth), 1)
-
-    def extract(j, carry):
-        bx, by, bz = corner(block_s[j], blocks_y, blocks_z)
-        wanted = lane - bz * 16
-        total = jnp.zeros((64, 256), F32)
-        for k in range(4):
-            if k < 3:
-                part = vel_v[k, bx, :, by]
-            else:
-                part = frac_v[bx, :, by].astype(BF16)
-            part = part.reshape(256, depth)
-            pick = jnp.where(wanted == column - 16 * k, 1.0, 0.0)
-            pick = jnp.where(column // 16 == k, pick, 0.0).astype(BF16)
-            total = total + lax.dot_general(
-                pick, part, (((1,), (1,)), ((), ())), preferred_element_type=F32
+        lax.fori_loop(0, drops, extract, 0, unroll=4)
+
+        for i in range(1, members):
+            peer = lax.rem(member + members - i, members)
+            pltpu.make_async_remote_copy(
+                src_ref=pack_v.at[peer],
+                dst_ref=got_v.at[peer],
+                send_sem=send_sem.at[i],
+                recv_sem=recv_sem.at[i],
+                device_id=(group, peer),
+                device_id_type=MESH,
+            ).wait_recv()
+
+        def pair_row(j, q):
+            both = got_v[owner_s[j], q]
+            return jnp.where(place_s[j] == 0, both[0:1], both[1:2])
+
+        def sample(j, carry):
+            row, deep = cell_parts(pair_row(j, 4))
+            picked = jnp.dot(block_v[j], hot_rows(row), preferred_element_type=F32)
+            hot = hot_depth(deep)
+            for q in range(4):
+                samp_v[j, q : q + 1] = jnp.sum(
+                    picked[16 * q : 16 * q + 16] * hot, axis=0, keepdims=True
+                )
+            return carry
+
+        lax.fori_loop(0, drops, sample, 0, unroll=4)
+        samp_v[drops, 0:3] = jnp.zeros((3, parcels), F32)
+        samp_v[drops, 3:4] = jnp.ones((1, parcels), F32)
+
+        def give(s, carry):
+            give_v[s // CAP, s % CAP] = samp_v[slot_s[s]].astype(BF16)
+            return carry
+
+        lax.fori_loop(0, members * CAP, give, 0, unroll=8)
+        for i in range(1, members):
+            peer = lax.rem(member + i, members)
+            copy = pltpu.make_async_remote_copy(
+                src_ref=give_v.at[peer],
+                dst_ref=back_ref.at[member],
+                send_sem=back_send.at[i],
+                recv_sem=back_recv.at[i],
+                device_id=(group, peer),
+                device_id_type=MESH,
             )
-        block_v[j] = total.astype(BF16)
+            copy.start()
+        back_ref[member] = give_v[member]
+
+        def scatter(j, carry):
+            row, deep = cell_parts(pair_row(j, 4))
+            hot = hot_depth(deep)
+            pull = pair_row(j, 3) * (1.0 - samp_v[j, 3:4])
+            parts = []
+            for q in range(3):
+                drag = pull * (samp_v[j, q : q + 1] - pair_row(j, q))
+                parts.append((drag.astype(BF16).astype(F32) * hot).astype(BF16))
+            spread = jnp.concatenate(parts, axis=0)
+            source = lax.dot_general(
+                hot_rows(row), spread, (((1,), (1,)), ((), ())), preferred_element_type=F32
+            )
+            source_ref[j] = source.astype(BF16)
+            return carry
+
+        lax.fori_loop(0, drops, scatter, 0, unroll=4)
+
+    edges(0)
+    fluxx_v[...] = flux(vel_v[0, 0, 3].astype(F32), frac_v[0, 3], frac_v[0, 4])
+
+    def plane(n, carry):
+        @pl.when(jnp.logical_and(lax.rem(n, 4) == 2, n < quads - 4))
+        def _():
+            edges(lax.div(n, 4) + 1)
+
+        @pl.when(n == quads - 6)
+        def _():
+            for copy in side_faces():
+                copy.start()
+            drag()
+
+        @pl.when(n == quads - 2)
+        def _():
+            for copy in faces + side_faces():
+                copy.wait()
+            frac_v[blocks_x, 0] = hxn_v[...] * high_x
+
+        @pl.when(n == quads - 1)
+        def _():
+            fluxx_v[...] = flux(hxu_v[...].astype(F32) * low_x, hxf_v[...], frac_v[0, 0])
+
+        quad(lax.rem(n + 1, quads))
         return carry
 
-    lax.fori_loop(0, drops, extract, 0, unroll=4)
-
-    for i in range(1, members):
-        peer = lax.rem(member + members - i, members)
-        pltpu.make_async_remote_copy(
-            src_ref=pack_v.at[peer],
-            dst_ref=got_v.at[peer],
-            send_sem=send_sem.at[i],
-            recv_sem=recv_sem.at[i],
-            device_id=(group, peer),
-            device_id_type=MESH,
-        ).wait_recv()
-
-    def pair_row(j, q):
-        both = got_v[owner_s[j], q]
-        return jnp.where(place_s[j] == 0, both[0:1], both[1:2])
-
-    def sample(j, carry):
-        row, deep = cell_parts(pair_row(j, 4))
-        picked = jnp.dot(block_v[j], hot_rows(row), preferred_element_type=F32)
-        hot = hot_depth(deep)
-        for q in range(4):
-            samp_v[j, q : q + 1] = jnp.sum(
-                picked[16 * q : 16 * q + 16] * hot, axis=0, keepdims=True
-            )
-        return carry
-
-    lax.fori_loop(0, drops, sample, 0, unroll=4)
-    samp_v[drops, 0:3] = jnp.zeros((3, parcels), F32)
-    samp_v[drops, 3:4] = jnp.ones((1, parcels), F32)
-
-    def give(s, carry):
-        give_v[s // CAP, s % CAP] = samp_v[slot_s[s]].astype(BF16)
-        return carry
-
-    lax.fori_loop(0, members * CAP, give, 0, unroll=8)
-    for i in range(1, members):
-        peer = lax.rem(member + i, members)
-        copy = pltpu.make_async_remote_copy(
-            src_ref=give_v.at[peer],
-            dst_ref=back_ref.at[member],
-            send_sem=back_send.at[i],
-            recv_sem=back_recv.at[i],
-            device_id=(group, peer),
-            device_id_type=MESH,
-        )
-        copy.start()
-        sends.append(copy)
-    back_ref[member] = give_v[member]
-
-    def scatter(j, carry):
-        row, deep = cell_parts(pair_row(j, 4))
-        hot = hot_depth(deep)
-        pull = pair_row(j, 3) * (1.0 - samp_v[j, 3:4])
-        parts = []
-        for q in range(3):
-            drag = pull * (samp_v[j, q : q + 1] - pair_row(j, q))
-            parts.append((drag.astype(BF16).astype(F32) * hot).astype(BF16))
-        spread = jnp.concatenate(parts, axis=0)
-        source = lax.dot_general(
-            hot_rows(row), spread, (((1,), (1,)), ((), ())), preferred_element_type=F32
-        )
-        source_ref[j] = source.astype(BF16)
-        return carry
-
-    lax.fori_loop(0, drops, scatter, 0, unroll=4)
-
-    for copy in faces:
-        copy.wait()
-    low_x = jnp.where(group > 0, 1.0, 0.0)
-    high_x = jnp.where(group < groups - 1, 1.0, 0.0)
-    low_y = jnp.where(member > 0, 1.0, 0.0)
-    high_y = jnp.where(member < members - 1, 1.0, 0.0)
-    frac_v[blocks_x, 0] = hxn_v[...] * high_x
-
-    def flux(speed, here, there):
-        return speed * jnp.where(speed > 0.0, here, there)
-
-    fluxx_v[...] = flux(hxu_v[...].astype(F32) * low_x, hxf_v[...], frac_v[0, 0])
-
-    def full(row):
-        return jnp.broadcast_to(row, (8, 128))
-
-    row_id = lax.broadcasted_iota(jnp.int32, (8, 128), 0)
-    lane_id = lax.broadcasted_iota(jnp.int32, (8, 128), 1)
-    first_row, last_row = row_id == 0, row_id == 7
-    first_lane, last_lane = lane_id == 0, lane_id == 127
-    halves = [slice(h * 128, h * 128 + 128) for h in range(depth // 128)]
-    tiles = blocks_y * 2
-
-    def split(row):
-        return [full(row[:, h]) for h in halves]
-
-    def one_plane(bx, x):
-        def at(t):
-            return t // 2, slice(8 * (t % 2), 8 * (t % 2) + 8)
-
-        def speeds(k, t):
-            pairs = [vel_v[k, bx, x, t, :, h].astype(F32) for h in halves]
-            return [[p[8 * i : 8 * i + 8] for p in pairs] for i in range(2)]
-
-        after = bx * 16 + x + 1
-        bn, xn = lax.div(after, 16), lax.rem(after, 16)
-        here = [[frac_v[(bx, x) + at(t) + (h,)] for h in halves] for t in range(tiles)]
-        behind = split(flux(hyu_v[bx, x] * low_y, hyf_v[bx, x], frac_v[bx, x, 0, 0:1, :]))
-        beyond = split(hyn_v[bx, x] * high_y)
-        rolled = [pltpu.roll(f, 7, 0) for f in here[0]]
-        for t in range(tiles):
-            if t % 2 == 0:
-                pair = [speeds(k, t // 2) for k in range(3)]
-            speed = [pair[k][t % 2] for k in range(3)]
-            if t + 1 < tiles:
-                rolled_next = [pltpu.roll(f, 7, 0) for f in here[t + 1]]
-            else:
-                rolled_next = beyond
-            lanes = [pltpu.roll(f, 127, 1) for f in here[t]] + [jnp.zeros((8, 128), F32)]
-            deep = [
-                flux(speed[2][i], here[t][i], jnp.where(last_lane, lanes[i + 1], lanes[i]))
-                for i in range(len(halves))
-            ]
-            turned = [jnp.zeros((8, 128), F32)] + [pltpu.roll(d, 1, 1) for d in deep]
-            for i, h in enumerate(halves):
-                spot = at(t) + (h,)
-                now = flux(speed[0][i], here[t][i], frac_v[(bn, xn) + spot])
-                change = now - fluxx_v[spot]
-                fluxx_v[spot] = now
-                ahead = jnp.where(last_row, rolled_next[i], rolled[i])
-                now = flux(speed[1][i], here[t][i], ahead)
-                moved = pltpu.roll(now, 1, 0)
-                change = change + (now - jnp.where(first_row, behind[i], moved))
-                behind[i] = moved
-                under = jnp.where(first_lane, turned[i], turned[i + 1])
-                change = change + (deep[i] - under)
-                next_v[(bx, x) + spot] = jnp.minimum(here[t][i] - COURANT * change, 1.0)
-            rolled = rolled_next
-
-    def plane(n, carry):
-        bx, x = lax.div(n, 4), lax.rem(n, 4) * 4
-        for i in range(4):
-            one_plane(bx, x + i)
-        return carry
-
-    lax.fori_loop(0, blocks_x * 4, plane, 0)
+    lax.fori_loop(0, quads, plane, 0)
+    lax.fori_loop(0, blocks_x * 16, mend, 0, unroll=8)
 
     for i in range(1, members):
         peer = lax.rem(member + members - i, members)
@@ -377,7 +417,7 @@
             recv_sem=back_recv.at[i],
             device_id=(group, peer),
             device_id_type=MESH,
-        ).wait_recv()
+        ).wait()
     for copy in sends:
         copy.wait_send()
 

time: 30.6 us -> 28 us (0.915)
  Pallas kernels: 29.5 us -> 27.2 us
    pallas_call x1, Pallas kernels: 23.5 us -> 21 us  [per_device(): pl.pallas_call(functools.partial(exchange_kernel, groups, members), out_s...]
where the time goes in v2:
time: 28 us; the launch traced here: 27.9 us
  Pallas kernels  27.2 us (97%)
  between operations  0.69 us (2%)
    pallas_call x1, Pallas kernels, per_device(): pl.pallas_call(functools.partial(exchange_kernel, groups, members), out_s...  21 us
    pallas_call x1, Pallas kernels, per_device(): pl.pallas_call(field_kernel, out_shape=(shaped(frac5.shape, F32), shaped(...  6.14 us

profile of v2, /device:TPU:0, one launch (start us, length us, event | category | flops | bytes accessed | tf_op | source)
XLA Modules:
  0.0 27.9 jit_solution(15004880188242581482)
XLA Ops:
  0.6 0.0 copy-start.1
  0.6 0.0 copy-start
  0.7 0.0 copy-start.2
  0.7 21.0 %exchange.1 = (bf16[3,4,16,4,16,256]{5,4,3,2,1,0:T(8,128)(2,1)S(1)}, f32[4,16,4,16,256]{4,3,2,1,0:T(8,128)S(1)}, bf16[16,256,48]{2,1,0:T(8,128)(2,1)S(1)}, bf16[16,2,4,512]{3,2,1,0:T(4,128)(2,1)S(1)}) custom-call(s32[16]{0:T(128)} %bitcast.19, s32[16]{0:T(128)} %bitcast.25, bf16[3,4,16,4,16,256]{5,4,3,2,1,0:T(8,128)(2,1)} %bitcast.21, ...), custom_call_target="tpu_custom_call" | custom-call | tf_op jit(solution)/shard_map/exchange/pallas_call | solution.py:558
  21.7 0.0 copy-done.1
  21.7 0.0 copy-done
  21.7 0.0 copy-done.2
  21.7 6.1 %field.1 = (f32[4,16,4,16,256]{4,3,2,1,0:T(8,128)}, bf16[3,4,16,4,16,256]{5,4,3,2,1,0:T(8,128)(2,1)}, f32[16,3,2,512]{3,2,1,0:T(2,128)}) custom-call(s32[16]{0:T(128)S(1)} %bitcast.20, bf16[3,4,16,4,16,256]{5,4,3,2,1,0:T(8,128)(2,1)S(1)} %get-tuple-element.10.vel_ref, f32[4,16,4,16,256]{4,3,2,1,0:T(8,128)S(1)} %get-tuple-element.11.next_ref, ...), custom_call_target="tpu_custom_call" | custom-call | tf_op jit(solution)/shard_map/field/pallas_call | solution.py:608
Async XLA Ops:
  0.6 21.1 %copy-start.1 = (f32[1,1,16,2,512]{4,3,2,1,0:T(2,128)S(1)}, f32[1,1,16,2,512]{4,3,2,1,0:T(2,128)}, u32[]{:S(2)}) copy-start(f32[1,1,16,2,512]{4,3,2,1,0:T(2,128)} %param.13) | copy-start | bytes 196612
  0.6 21.1 %copy-start = (f32[1,1,16,2,3,512]{5,3,4,2,1,0:T(2,128)S(1)}, f32[1,1,16,2,3,512]{5,3,4,2,1,0:T(2,128)}, u32[]{:S(2)}) copy-start(f32[1,1,16,2,3,512]{5,3,4,2,1,0:T(2,128)} %param.12) | copy-start | bytes 589828
  0.7 21.1 %copy-start.2 = (s32[1,1,16]{2,1,0:T(1,128)S(1)}, s32[1,1,16]{2,1,0:T(1,128)}, u32[]{:S(2)}) copy-start(s32[1,1,16]{2,1,0:T(1,128)} %param.10) | copy-start | bytes 196

commit v3 on v2

--- a/solution.py
+++ b/solution.py
@@ -112,7 +112,7 @@
     ]
     for copy in names + parcel_loads:
         copy.start()
-    for c in range(blocks_x):
+    for c in range(2):
         for copy in chunk_loads(c):
             copy.start()
 
@@ -234,6 +234,11 @@
         for copy in chunk_loads(c):
             copy.wait()
 
+        @pl.when(c + 2 < blocks_x)
+        def _():
+            for copy in chunk_loads(c + 2):
+                copy.start()
+
         def edge(x, carry):
             syf_v[c, x] = frac_v[c, x, blocks_y - 1, 15:16, :]
             syn_v[c, x] = frac_v[c, x, 0, 0:1, :]
@@ -241,23 +246,6 @@
             return carry
 
         lax.fori_loop(0, 16, edge, 0, unroll=8)
-
-    pl.semaphore_wait(barrier, members + 1)
-
-    sends = []
-    for i in range(1, members):
-        peer = lax.rem(member + i, members)
-        copy = pltpu.make_async_remote_copy(
-            src_ref=pack_v.at[peer],
-            dst_ref=got_v.at[member],
-            send_sem=send_sem.at[i],
-            recv_sem=recv_sem.at[i],
-            device_id=(group, peer),
-            device_id_type=MESH,
-        )
-        copy.start()
-        sends.append(copy)
-    got_v[member] = pack_v[member]
 
     def face(src, dst, number, device):
         copy = pltpu.make_async_remote_copy(
@@ -270,13 +258,30 @@
         )
         return copy
 
-    faces = [
-        face(vel_hbm.at[0, blocks_x - 1, 15], hxu_v, 0, (up, member)),
-        face(frac_hbm.at[blocks_x - 1, 15], hxf_v, 1, (up, member)),
-        face(frac_hbm.at[0, 0], hxn_v, 2, (down, member)),
-    ]
-    for copy in faces:
-        copy.start()
+    def end_faces():
+        return [
+            face(vel_hbm.at[0, blocks_x - 1, 15], hxu_v, 0, (up, member)),
+            face(frac_hbm.at[blocks_x - 1, 15], hxf_v, 1, (up, member)),
+            face(frac_hbm.at[0, 0], hxn_v, 2, (down, member)),
+        ]
+
+    def send_out():
+        pl.semaphore_wait(barrier, members + 1)
+
+        for i in range(1, members):
+            peer = lax.rem(member + i, members)
+            copy = pltpu.make_async_remote_copy(
+                src_ref=pack_v.at[peer],
+                dst_ref=got_v.at[member],
+                send_sem=send_sem.at[i],
+                recv_sem=recv_sem.at[i],
+                device_id=(group, peer),
+                device_id_type=MESH,
+            )
+            copy.start()
+        got_v[member] = pack_v[member]
+        for copy in end_faces():
+            copy.start()
 
     def side_faces():
         return [
@@ -312,7 +317,7 @@
             block_v[j] = total.astype(BF16)
             return carry
 
-        lax.fori_loop(0, drops, extract, 0, unroll=4)
+        lax.fori_loop(0, drops, extract, 0, unroll=8)
 
         for i in range(1, members):
             peer = lax.rem(member + members - i, members)
@@ -323,7 +328,7 @@
                 recv_sem=recv_sem.at[i],
                 device_id=(group, peer),
                 device_id_type=MESH,
-            ).wait_recv()
+            ).wait()
 
         def pair_row(j, q):
             both = got_v[owner_s[j], q]
@@ -339,7 +344,7 @@
                 )
             return carry
 
-        lax.fori_loop(0, drops, sample, 0, unroll=4)
+        lax.fori_loop(0, drops, sample, 0, unroll=8)
         samp_v[drops, 0:3] = jnp.zeros((3, parcels), F32)
         samp_v[drops, 3:4] = jnp.ones((1, parcels), F32)
 
@@ -347,7 +352,7 @@
             give_v[s // CAP, s % CAP] = samp_v[slot_s[s]].astype(BF16)
             return carry
 
-        lax.fori_loop(0, members * CAP, give, 0, unroll=8)
+        lax.fori_loop(0, members * CAP, give, 0, unroll=16)
         for i in range(1, members):
             peer = lax.rem(member + i, members)
             copy = pltpu.make_async_remote_copy(
@@ -376,9 +381,11 @@
             source_ref[j] = source.astype(BF16)
             return carry
 
-        lax.fori_loop(0, drops, scatter, 0, unroll=4)
-
-    edges(0)
+        lax.fori_loop(0, drops, scatter, 0, unroll=8)
+
+    send_out()
+
+    edges(jnp.int32(0))
     fluxx_v[...] = flux(vel_v[0, 0, 3].astype(F32), frac_v[0, 3], frac_v[0, 4])
 
     def plane(n, carry):
@@ -390,11 +397,14 @@
         def _():
             for copy in side_faces():
                 copy.start()
+
+        @pl.when(n == quads - 6)
+        def _():
             drag()
 
         @pl.when(n == quads - 2)
         def _():
-            for copy in faces + side_faces():
+            for copy in end_faces() + side_faces():
                 copy.wait()
             frac_v[blocks_x, 0] = hxn_v[...] * high_x
 
@@ -406,7 +416,7 @@
         return carry
 
     lax.fori_loop(0, quads, plane, 0)
-    lax.fori_loop(0, blocks_x * 16, mend, 0, unroll=8)
+    lax.fori_loop(0, blocks_x * 16, mend, 0, unroll=16)
 
     for i in range(1, members):
         peer = lax.rem(member + members - i, members)
@@ -418,8 +428,6 @@
             device_id=(group, peer),
             device_id_type=MESH,
         ).wait()
-    for copy in sends:
-        copy.wait_send()
 
 
 def field_kernel(
@@ -434,6 +442,7 @@
     vel_out,
     pv_out,
     fresh_v,
+    pv_v,
     lead_s,
     store_sem,
     block_sem,
@@ -447,8 +456,23 @@
         for c in range(blocks_x)
     ]
     frac_copy = pltpu.make_async_copy(next_ref, frac_out, store_sem.at[blocks_x])
-    for copy in bulk + [frac_copy]:
+    for copy in bulk:
         copy.start()
+
+    def gain_pair(owner, carry):
+        sampled = [back_ref[owner, place].astype(F32) for place in range(CAP)]
+        rate = pr_ref[owner]
+        old = pv_ref[owner]
+        share = jnp.concatenate([s[3:4] for s in sampled], axis=0)
+        pull = rate * (1.0 - share)
+        for q in range(3):
+            speed = jnp.concatenate([s[q : q + 1] for s in sampled], axis=0)
+            pv_v[owner, q] = old[q] + pull * (speed - old[q])
+        return carry
+
+    lax.fori_loop(0, members, gain_pair, 0, unroll=4)
+    pv_copy = pltpu.make_async_copy(pv_v, pv_out, store_sem.at[blocks_x + 1])
+    pv_copy.start()
 
     keys = [lax.div(block_s[j], 8) for j in range(drops)]
     for j in range(drops):
@@ -468,7 +492,7 @@
             fresh_v[j, k] = vel_ref[k, bx, :, by, :, lanes]
         return carry
 
-    lax.fori_loop(0, drops, begin, 0, unroll=4)
+    lax.fori_loop(0, drops, begin, 0, unroll=8)
 
     lane = lax.broadcasted_iota(jnp.int32, (48, 128), 1)
     column = lax.broadcasted_iota(jnp.int32, (48, 128), 0)
@@ -486,7 +510,7 @@
             fresh_v[lead, k] = (old + moved).astype(BF16).reshape(16, 16, 128)
         return carry
 
-    lax.fori_loop(0, drops, patch, 0, unroll=4)
+    lax.fori_loop(0, drops, patch, 0, unroll=8)
 
     def block_copy(j):
         bx, by, lanes, _ = spot(j)
@@ -494,6 +518,7 @@
             fresh_v.at[j], vel_out.at[:, bx, :, by, :, lanes], block_sem.at[j]
         )
 
+    frac_copy.start()
     for copy in bulk:
         copy.wait()
     for j in range(drops):
@@ -502,19 +527,8 @@
         def _():
             block_copy(j).start()
 
-    def gain_pair(owner, carry):
-        sampled = [back_ref[owner, place].astype(F32) for place in range(CAP)]
-        rate = pr_ref[owner]
-        old = pv_ref[owner]
-        share = jnp.concatenate([s[3:4] for s in sampled], axis=0)
-        pull = rate * (1.0 - share)
-        for q in range(3):
-            speed = jnp.concatenate([s[q : q + 1] for s in sampled], axis=0)
-            pv_out[owner, q] = old[q] + pull * (speed - old[q])
-        return carry
-
-    lax.fori_loop(0, members, gain_pair, 0, unroll=4)
     frac_copy.wait()
+    pv_copy.wait()
     for j in range(drops):
 
         @pl.when(lead_s[j] == j)
@@ -613,11 +627,12 @@
                 shaped(pv.shape, F32),
             ),
             in_specs=[smem] + [vmem] * 6,
-            out_specs=(hbm, hbm, vmem),
+            out_specs=(hbm, hbm, hbm),
             scratch_shapes=[
                 pltpu.VMEM((drops, 3, 16, 16, 128), BF16),
+                pltpu.VMEM(pv.shape, F32),
                 pltpu.SMEM((drops,), jnp.int32),
-                pltpu.SemaphoreType.DMA((blocks_x + 1,)),
+                pltpu.SemaphoreType.DMA((blocks_x + 2,)),
                 pltpu.SemaphoreType.DMA((drops,)),
             ],
             compiler_params=pltpu.CompilerParams(vmem_limit_bytes=40 << 20),

time: 28 us -> 26.7 us (0.954)
  Pallas kernels: 27.2 us -> 25.9 us
    pallas_call x1, Pallas kernels: 21 us -> 20.4 us  [per_device(): pl.pallas_call(functools.partial(exchange_kernel, groups, members), out_s...]
    pallas_call x1, Pallas kernels: 6.14 us -> 5.53 us  [per_device(): pl.pallas_call(field_kernel, out_shape=(shaped(frac5.shape, F32), shaped(...]
where the time goes in v3:
time: 26.7 us; the launch traced here: 26.6 us
  Pallas kernels  25.9 us (97%)
  between operations  0.69 us (3%)
    pallas_call x1, Pallas kernels, per_device(): pl.pallas_call(functools.partial(exchange_kernel, groups, members), out_s...  20.4 us
    pallas_call x1, Pallas kernels, per_device(): pl.pallas_call(field_kernel, out_shape=(shaped(frac5.shape, F32), shaped(...  5.53 us

profile of v3, /device:TPU:0, one launch (start us, length us, event | category | flops | bytes accessed | tf_op | source)
XLA Modules:
  0.0 26.6 jit_solution(8184550104494182727)
XLA Ops:
  0.6 0.0 copy-start.1
  0.6 0.0 copy-start
  0.7 0.0 copy-start.2
  0.7 20.4 %exchange.1 = (bf16[3,4,16,4,16,256]{5,4,3,2,1,0:T(8,128)(2,1)S(1)}, f32[4,16,4,16,256]{4,3,2,1,0:T(8,128)S(1)}, bf16[16,256,48]{2,1,0:T(8,128)(2,1)S(1)}, bf16[16,2,4,512]{3,2,1,0:T(4,128)(2,1)S(1)}) custom-call(s32[16]{0:T(128)} %bitcast.19, s32[16]{0:T(128)} %bitcast.25, bf16[3,4,16,4,16,256]{5,4,3,2,1,0:T(8,128)(2,1)} %bitcast.21, ...), custom_call_target="tpu_custom_call" | custom-call | tf_op jit(solution)/shard_map/exchange/pallas_call | solution.py:572
  21.0 0.0 copy-done.1
  21.0 0.0 copy-done
  21.1 0.0 copy-done.2
  21.1 5.5 %field.1 = (f32[4,16,4,16,256]{4,3,2,1,0:T(8,128)}, bf16[3,4,16,4,16,256]{5,4,3,2,1,0:T(8,128)(2,1)}, f32[16,3,2,512]{3,2,1,0:T(2,128)}) custom-call(s32[16]{0:T(128)S(1)} %bitcast.20, bf16[3,4,16,4,16,256]{5,4,3,2,1,0:T(8,128)(2,1)S(1)} %get-tuple-element.10.vel_ref, f32[4,16,4,16,256]{4,3,2,1,0:T(8,128)S(1)} %get-tuple-element.11.next_ref, ...), custom_call_target="tpu_custom_call" | custom-call | tf_op jit(solution)/shard_map/field/pallas_call | solution.py:622
Async XLA Ops:
  0.6 20.4 %copy-start.1 = (f32[1,1,16,2,512]{4,3,2,1,0:T(2,128)S(1)}, f32[1,1,16,2,512]{4,3,2,1,0:T(2,128)}, u32[]{:S(2)}) copy-start(f32[1,1,16,2,512]{4,3,2,1,0:T(2,128)} %param.13) | copy-start | bytes 196612
  0.6 20.4 %copy-start = (f32[1,1,16,2,3,512]{5,3,4,2,1,0:T(2,128)S(1)}, f32[1,1,16,2,3,512]{5,3,4,2,1,0:T(2,128)}, u32[]{:S(2)}) copy-start(f32[1,1,16,2,3,512]{5,3,4,2,1,0:T(2,128)} %param.12) | copy-start | bytes 589828
  0.7 20.4 %copy-start.2 = (s32[1,1,16]{2,1,0:T(1,128)S(1)}, s32[1,1,16]{2,1,0:T(1,128)}, u32[]{:S(2)}) copy-start(s32[1,1,16]{2,1,0:T(1,128)} %param.10) | copy-start | bytes 196

commit v4 on v3

--- a/solution.py
+++ b/solution.py
@@ -290,7 +290,7 @@
             face(syn_v, hyn_v, 5, (group, left)),
         ]
 
-    def drag():
+    def collect():
         column = lax.broadcasted_iota(jnp.int32, (64, 128), 0)
         lane = lax.broadcasted_iota(jnp.int32, (64, 128), 1)
 
@@ -319,6 +319,8 @@
 
         lax.fori_loop(0, drops, extract, 0, unroll=8)
 
+    def drag():
+
         for i in range(1, members):
             peer = lax.rem(member + members - i, members)
             pltpu.make_async_remote_copy(
@@ -399,6 +401,10 @@
                 copy.start()
 
         @pl.when(n == quads - 6)
+        def _():
+            collect()
+
+        @pl.when(n == quads - 4)
         def _():
             drag()
 

time: 26.7 us -> 26.7 us (level)
  no operation moved by 1% of the time
where the time goes in v4:
time: 26.7 us; the launch traced here: 26.5 us
  Pallas kernels  25.8 us (97%)
  between operations  0.69 us (3%)
    pallas_call x1, Pallas kernels, per_device(): pl.pallas_call(functools.partial(exchange_kernel, groups, members), out_s...  20.4 us
    pallas_call x1, Pallas kernels, per_device(): pl.pallas_call(field_kernel, out_shape=(shaped(frac5.shape, F32), shaped(...  5.41 us

profile of v4, /device:TPU:0, one launch (start us, length us, event | category | flops | bytes accessed | tf_op | source)
XLA Modules:
  0.0 26.5 jit_solution(12287136191819683883)
XLA Ops:
  0.6 0.0 copy-start.1
  0.6 0.0 copy-start
  0.7 0.0 copy-start.2
  0.7 20.4 %exchange.1 = (bf16[3,4,16,4,16,256]{5,4,3,2,1,0:T(8,128)(2,1)S(1)}, f32[4,16,4,16,256]{4,3,2,1,0:T(8,128)S(1)}, bf16[16,256,48]{2,1,0:T(8,128)(2,1)S(1)}, bf16[16,2,4,512]{3,2,1,0:T(4,128)(2,1)S(1)}) custom-call(s32[16]{0:T(128)} %bitcast.19, s32[16]{0:T(128)} %bitcast.25, bf16[3,4,16,4,16,256]{5,4,3,2,1,0:T(8,128)(2,1)} %bitcast.21, ...), custom_call_target="tpu_custom_call" | custom-call | tf_op jit(solution)/shard_map/exchange/pallas_call | solution.py:578
  21.0 0.0 copy-done.1
  21.0 0.0 copy-done
  21.1 0.0 copy-done.2
  21.1 5.4 %field.1 = (f32[4,16,4,16,256]{4,3,2,1,0:T(8,128)}, bf16[3,4,16,4,16,256]{5,4,3,2,1,0:T(8,128)(2,1)}, f32[16,3,2,512]{3,2,1,0:T(2,128)}) custom-call(s32[16]{0:T(128)S(1)} %bitcast.20, bf16[3,4,16,4,16,256]{5,4,3,2,1,0:T(8,128)(2,1)S(1)} %get-tuple-element.10.vel_ref, f32[4,16,4,16,256]{4,3,2,1,0:T(8,128)S(1)} %get-tuple-element.11.next_ref, ...), custom_call_target="tpu_custom_call" | custom-call | tf_op jit(solution)/shard_map/field/pallas_call | solution.py:628
Async XLA Ops:
  0.6 20.4 %copy-start.1 = (f32[1,1,16,2,512]{4,3,2,1,0:T(2,128)S(1)}, f32[1,1,16,2,512]{4,3,2,1,0:T(2,128)}, u32[]{:S(2)}) copy-start(f32[1,1,16,2,512]{4,3,2,1,0:T(2,128)} %param.13) | copy-start | bytes 196612
  0.6 20.4 %copy-start = (f32[1,1,16,2,3,512]{5,3,4,2,1,0:T(2,128)S(1)}, f32[1,1,16,2,3,512]{5,3,4,2,1,0:T(2,128)}, u32[]{:S(2)}) copy-start(f32[1,1,16,2,3,512]{5,3,4,2,1,0:T(2,128)} %param.12) | copy-start | bytes 589828
  0.7 20.4 %copy-start.2 = (s32[1,1,16]{2,1,0:T(1,128)S(1)}, s32[1,1,16]{2,1,0:T(1,128)}, u32[]{:S(2)}) copy-start(s32[1,1,16]{2,1,0:T(1,128)} %param.10) | copy-start | bytes 196
